TPU v7x, 32 devices: a whole 2x2x4 slice. The times are simulated.
32 devices in a mesh: expert: 4 (over y, core), fsdp: 8 (over z, x).
Axes of the slice: x: 2, y: 2, z: 4, core: 2. Of those that a mesh axis runs over, the one named last changes fastest.
Arguments:
- layer_input: bfloat16 [8192, 2048], P(('expert', 'fsdp')), may hold values from -6 to 6
- expert_ids: int32 [8192, 8], P(('expert', 'fsdp')), may hold values from 0 to 15, as said below
- slot_ids: int32 [8192, 8], P(('expert', 'fsdp')), may hold values from 0 to 255, as said below
- attn_gain: float32 [2048], replicated, may hold values from 0.25 to 1.75
- qkv_weight: bfloat16 [2048, 6144], P('fsdp'), may hold values from -0.125 to 0.125
- query_gain: float32 [128], replicated, may hold values from 0.25 to 1.75
- key_gain: float32 [128], replicated, may hold values from 0.25 to 1.75
- out_weight: bfloat16 [2048, 2048], P('fsdp'), may hold values from -1 to 1
- ffn_gain: float32 [2048], replicated, may hold values from 0.25 to 1.75
- router_weight: bfloat16 [2048, 16], P('fsdp'), may hold values from -0.0625 to 0.0625
- gate_up_weight: bfloat16 [16, 2048, 2048], P('expert', 'fsdp'), may hold values from -0.125 to 0.125
- down_weight: bfloat16 [16, 1024, 2048], P('expert', 'fsdp'), may hold values from -0.75 to 0.75
- cotangent: bfloat16 [8192, 2048], P(('expert', 'fsdp')), may hold values from -6 to 6
Outputs:
- mixed_out: bfloat16 [8192, 2048], P(('expert', 'fsdp'))
- input_grad: float32 [8192, 2048], P(('expert', 'fsdp'))
- attn_gain_grad: float32 [2048], replicated
- qkv_weight_grad: float32 [2048, 6144], P('fsdp')
- query_gain_grad: float32 [128], replicated
- key_gain_grad: float32 [128], replicated
- out_weight_grad: float32 [2048, 2048], P('fsdp')
- ffn_gain_grad: float32 [2048], replicated
- router_weight_grad: float32 [2048, 16], P('fsdp')
- gate_up_grad: float32 [16, 2048, 2048], P('expert', 'fsdp')
- down_grad: float32 [16, 1024, 2048], P('expert', 'fsdp')
Inputs may be any that keep to these rules, and one draw needn't show every extreme that they name: `expert_ids`: each row names 8 different experts. Among the 256 rows of one device no expert is named more than 256 times; in every device's rows one expert is named exactly 256 times. `slot_ids`: among the rows of one device, the routes to one expert have different slots.
All inputs are finite; a program needn't handle non-finite values.
Results may differ from a plain program's by a relative error of at most 0.022.
Values may be sent and summed in bfloat16 or wider, within the bound.
No kernel may reach another device: no remote copies, remote signals or barrier semaphores. Data moves between devices by JAX's collectives and lax.ppermute only.
A program may use at most 384 MiB of HBM per device.

v0:
```python
import jax
import jax.numpy as jnp
from jax import lax
from jax.sharding import PartitionSpec as P

EPSILON = 1e-06
ROPE_BASE = 50000.0


def normalize(values):
    factor = lax.rsqrt(jnp.mean(values * values, -1, keepdims=True) + EPSILON)
    return (values * factor, factor)


def norm_back(grad_unit, unit_val, factor):
    return factor * (grad_unit - unit_val * jnp.mean(grad_unit * unit_val, -1, keepdims=True))


def tables(length, head_size):
    half_size = head_size // 2
    frequency = ROPE_BASE ** (-(jnp.arange(half_size, dtype=jnp.float32) * 2.0 / head_size))
    angles = jnp.arange(length, dtype=jnp.float32)[:, None] * frequency[None, :]
    angles = jnp.concatenate([angles, angles], 1)
    return (jnp.cos(angles)[:, None, :], jnp.sin(angles)[:, None, :])


def rotate(values, cos_table, sine_table):
    half_size = values.shape[-1] // 2
    turned = jnp.concatenate([-values[..., half_size:], values[..., :half_size]], -1)
    return values * cos_table + turned * sine_table


def rotate_back(gradient, cos_table, sine_table):
    half_size = gradient.shape[-1] // 2
    turned_grad = gradient * sine_table
    return gradient * cos_table + jnp.concatenate(
        [turned_grad[..., half_size:], -turned_grad[..., :half_size]], -1
    )


def local(
    layer_input,
    expert_ids,
    slot_ids,
    attn_gain,
    qkv_weight,
    query_gain,
    key_gain,
    out_weight,
    ffn_gain,
    router_weight,
    gate_up_weight,
    down_weight,
    cotangent,
):
    tokens, model_width = layer_input.shape
    top_count = expert_ids.shape[1]
    head_size = query_gain.shape[0]
    head_count = model_width // head_size
    experts = router_weight.shape[1]
    hidden = gate_up_weight.shape[2] // 2
    capacity = 2 * tokens * top_count // experts
    score_scale = head_size ** (-0.5)
    source = layer_input.astype(jnp.float32)
    unit_one, factor_one = normalize(source)
    normed = (unit_one * attn_gain).astype(jnp.bfloat16)
    qkv_full, out_full, router_full = (
        lax.all_gather(qkv_weight, "fsdp", axis=0, tiled=True),
        lax.all_gather(out_weight, "fsdp", axis=0, tiled=True),
        lax.all_gather(router_weight, "fsdp", axis=0, tiled=True),
    )
    projected = jnp.dot(normed, qkv_full, preferred_element_type=jnp.float32)
    queries = projected[:, :model_width].reshape(tokens, head_count, head_size)
    keys_raw = projected[:, model_width : 2 * model_width].reshape(tokens, head_count, head_size)
    values_raw = projected[:, 2 * model_width :].reshape(tokens, head_count, head_size)
    unit_query, factor_query = normalize(queries)
    unit_key, factor_key = normalize(keys_raw)
    cos_table, sine_table = tables(tokens, head_size)
    query_rot = rotate(unit_query * query_gain, cos_table, sine_table).astype(jnp.bfloat16)
    key_rot = rotate(unit_key * key_gain, cos_table, sine_table).astype(jnp.bfloat16)
    value_low = values_raw.astype(jnp.bfloat16)
    scores = (
        jnp.einsum("qhd,khd->hqk", query_rot, key_rot, preferred_element_type=jnp.float32)
        * score_scale
    )
    top_score = jnp.max(scores, -1, keepdims=True)
    weights_raw = jnp.exp(scores - top_score)
    totals = jnp.sum(weights_raw, -1, keepdims=True)
    log_total = top_score + jnp.log(totals)
    prob_low = (weights_raw / totals).astype(jnp.bfloat16)
    mixed_heads = jnp.einsum(
        "hqk,khd->qhd", prob_low, value_low, preferred_element_type=jnp.float32
    )
    mixed_low = mixed_heads.reshape(tokens, model_width).astype(jnp.bfloat16)
    residual = source + jnp.dot(mixed_low, out_full, preferred_element_type=jnp.float32)
    unit_two, factor_two = normalize(residual)
    normed_two = (unit_two * ffn_gain).astype(jnp.bfloat16)
    logits = jnp.dot(normed_two, router_full, preferred_element_type=jnp.float32)
    onehot = (expert_ids[:, :, None] == jnp.arange(experts, dtype=jnp.int32)[None, None, :]).astype(
        jnp.float32
    )
    chosen = jnp.sum(onehot * logits[:, None, :], -1)
    gate_probs = jax.nn.softmax(chosen, -1)
    slot_index = (expert_ids * capacity + slot_ids).reshape(-1)
    copies = jnp.broadcast_to(normed_two[:, None, :], (tokens, top_count, model_width)).reshape(
        tokens * top_count, model_width
    )
    outgoing = jnp.zeros((experts * capacity, model_width), jnp.bfloat16).at[slot_index].set(copies)
    arrived = lax.all_to_all(
        outgoing.reshape(experts, capacity, model_width),
        "expert",
        split_axis=0,
        concat_axis=1,
        tiled=True,
    )
    gate_up_full, down_full = (
        lax.all_gather(gate_up_weight, "fsdp", axis=1, tiled=True),
        lax.all_gather(down_weight, "fsdp", axis=1, tiled=True),
    )
    gate_up_val = jnp.einsum(
        "erd,edf->erf", arrived, gate_up_full, preferred_element_type=jnp.float32
    )
    gate_part = gate_up_val[..., :hidden]
    up_part = gate_up_val[..., hidden:]
    sigmoid_gate = jax.nn.sigmoid(gate_part)
    activated = (gate_part * sigmoid_gate * up_part).astype(jnp.bfloat16)
    expert_out = jnp.einsum(
        "erf,efd->erd", activated, down_full, preferred_element_type=jnp.float32
    ).astype(jnp.bfloat16)
    returned = lax.all_to_all(
        expert_out, "expert", split_axis=1, concat_axis=0, tiled=True
    ).reshape(experts * capacity, model_width)
    picked = returned[slot_index].reshape(tokens, top_count, model_width).astype(jnp.float32)
    moe_sum = jnp.sum(gate_probs[:, :, None] * picked, 1)
    mixed_out = (residual + moe_sum).astype(jnp.bfloat16)
    upstream = cotangent.astype(jnp.float32)
    gate_grad = jnp.sum(picked * upstream[:, None, :], -1)
    row_grad = (
        (gate_probs[:, :, None] * upstream[:, None, :])
        .astype(jnp.bfloat16)
        .reshape(tokens * top_count, model_width)
    )
    grad_out = (
        jnp.zeros((experts * capacity, model_width), jnp.bfloat16).at[slot_index].set(row_grad)
    )
    grad_arrived = lax.all_to_all(
        grad_out.reshape(experts, capacity, model_width),
        "expert",
        split_axis=0,
        concat_axis=1,
        tiled=True,
    )
    gate_up_back, down_back = (
        lax.all_gather(gate_up_weight, "fsdp", axis=1, tiled=True),
        lax.all_gather(down_weight, "fsdp", axis=1, tiled=True),
    )
    act_grad = jnp.einsum(
        "erd,efd->erf", grad_arrived, down_back, preferred_element_type=jnp.float32
    )
    down_grad_full = jnp.einsum(
        "erf,erd->efd", activated, grad_arrived, preferred_element_type=jnp.float32
    )
    gate_grad_part = act_grad * up_part * sigmoid_gate * (1.0 + gate_part * (1.0 - sigmoid_gate))
    up_grad_part = act_grad * gate_part * sigmoid_gate
    both_grad = jnp.concatenate([gate_grad_part, up_grad_part], -1).astype(jnp.bfloat16)
    gate_up_grad_full = jnp.einsum(
        "erd,erf->edf", arrived, both_grad, preferred_element_type=jnp.float32
    )
    input_rows = jnp.einsum(
        "erf,edf->erd", both_grad, gate_up_back, preferred_element_type=jnp.float32
    ).astype(jnp.bfloat16)
    rows_back = lax.all_to_all(
        input_rows, "expert", split_axis=1, concat_axis=0, tiled=True
    ).reshape(experts * capacity, model_width)
    gate_up_grad, down_grad = (
        lax.psum_scatter(
            gate_up_grad_full.astype(jnp.bfloat16), "fsdp", scatter_dimension=1, tiled=True
        ).astype(jnp.float32),
        lax.psum_scatter(
            down_grad_full.astype(jnp.bfloat16), "fsdp", scatter_dimension=1, tiled=True
        ).astype(jnp.float32),
    )
    mean_grad = jnp.sum(gate_probs * gate_grad, -1, keepdims=True)
    chosen_grad = gate_probs * (gate_grad - mean_grad)
    logit_grad = jnp.sum(onehot * chosen_grad[:, :, None], 1).astype(jnp.bfloat16)
    router_grad_full = jnp.dot(normed_two.T, logit_grad, preferred_element_type=jnp.float32)
    routed_back = jnp.sum(
        rows_back[slot_index].reshape(tokens, top_count, model_width).astype(jnp.float32), 1
    )
    normed_two_grad = routed_back + jnp.dot(
        logit_grad, router_full.T, preferred_element_type=jnp.float32
    )
    ffn_gain_part = jnp.sum(normed_two_grad * unit_two, 0)
    residual_grad = upstream + norm_back(normed_two_grad * ffn_gain, unit_two, factor_two)
    attn_grad_low = residual_grad.astype(jnp.bfloat16)
    out_grad_full = jnp.dot(mixed_low.T, attn_grad_low, preferred_element_type=jnp.float32)
    mixed_grad = jnp.dot(attn_grad_low, out_full.T, preferred_element_type=jnp.float32).astype(
        jnp.bfloat16
    )
    mixed_grad = mixed_grad.reshape(tokens, head_count, head_size)
    value_grad = jnp.einsum(
        "hqk,qhd->khd", prob_low, mixed_grad, preferred_element_type=jnp.float32
    )
    prob_grad = jnp.einsum(
        "qhd,khd->hqk", mixed_grad, value_low, preferred_element_type=jnp.float32
    )
    scores_again = (
        jnp.einsum("qhd,khd->hqk", query_rot, key_rot, preferred_element_type=jnp.float32)
        * score_scale
    )
    prob_full = jnp.exp(scores_again - log_total)
    score_grad = (
        prob_full * (prob_grad - jnp.sum(prob_full * prob_grad, -1, keepdims=True))
    ).astype(jnp.bfloat16)
    query_grad = (
        jnp.einsum("hqk,khd->qhd", score_grad, key_rot, preferred_element_type=jnp.float32)
        * score_scale
    )
    key_grad = (
        jnp.einsum("hqk,qhd->khd", score_grad, query_rot, preferred_element_type=jnp.float32)
        * score_scale
    )
    query_grad = rotate_back(query_grad, cos_table, sine_table)
    key_grad = rotate_back(key_grad, cos_table, sine_table)
    query_gain_part = jnp.sum(query_grad * unit_query, (0, 1))
    key_gain_part = jnp.sum(key_grad * unit_key, (0, 1))
    query_pre = norm_back(query_grad * query_gain, unit_query, factor_query)
    key_pre = norm_back(key_grad * key_gain, unit_key, factor_key)
    qkv_grad_low = jnp.concatenate(
        [
            query_pre.reshape(tokens, model_width),
            key_pre.reshape(tokens, model_width),
            value_grad.reshape(tokens, model_width),
        ],
        1,
    ).astype(jnp.bfloat16)
    qkv_grad_full = jnp.dot(normed.T, qkv_grad_low, preferred_element_type=jnp.float32)
    normed_grad = jnp.dot(qkv_grad_low, qkv_full.T, preferred_element_type=jnp.float32)
    attn_gain_part = jnp.sum(normed_grad * unit_one, 0)
    input_grad = residual_grad + norm_back(normed_grad * attn_gain, unit_one, factor_one)
    qkv_shard, out_shard, router_shard = (
        lax.psum_scatter(
            qkv_grad_full.astype(jnp.bfloat16), "fsdp", scatter_dimension=0, tiled=True
        ).astype(jnp.float32),
        lax.psum_scatter(
            out_grad_full.astype(jnp.bfloat16), "fsdp", scatter_dimension=0, tiled=True
        ).astype(jnp.float32),
        lax.psum_scatter(
            router_grad_full.astype(jnp.bfloat16), "fsdp", scatter_dimension=0, tiled=True
        ).astype(jnp.float32),
    )
    qkv_weight_grad, out_weight_grad, router_weight_grad = (
        lax.psum(qkv_shard.astype(jnp.bfloat16), "expert").astype(jnp.float32),
        lax.psum(out_shard.astype(jnp.bfloat16), "expert").astype(jnp.float32),
        lax.psum(router_shard.astype(jnp.bfloat16), "expert").astype(jnp.float32),
    )
    attn_gain_grad, query_gain_grad, key_gain_grad, ffn_gain_grad = lax.psum(
        (attn_gain_part, query_gain_part, key_gain_part, ffn_gain_part), ("expert", "fsdp")
    )
    return (
        mixed_out,
        input_grad,
        attn_gain_grad,
        qkv_weight_grad,
        query_gain_grad,
        key_gain_grad,
        out_weight_grad,
        ffn_gain_grad,
        router_weight_grad,
        gate_up_grad,
        down_grad,
    )


def solution(mesh):
    return jax.shard_map(
        local,
        mesh=mesh,
        in_specs=(
            P(("expert", "fsdp"), None),
            P(("expert", "fsdp"), None),
            P(("expert", "fsdp"), None),
            P(),
            P("fsdp", None),
            P(),
            P(),
            P("fsdp", None),
            P(),
            P("fsdp", None),
            P("expert", "fsdp", None),
            P("expert", "fsdp", None),
            P(("expert", "fsdp"), None),
        ),
        out_specs=(
            P(("expert", "fsdp"), None),
            P(("expert", "fsdp"), None),
            P(),
            P("fsdp", None),
            P(),
            P(),
            P("fsdp", None),
            P(),
            P("fsdp", None),
            P("expert", "fsdp", None),
            P("expert", "fsdp", None),
        ),
        check_vma=False,
    )
```

profile of v0, /device:TPU:0, one launch (start us, length us, event | category | flops | bytes accessed | tf_op | source)
XLA Modules:
  0.0 3566.6 jit_solution(18210329636455333657)
XLA Ops:
  9.7 1.5 convert_element_type.132
  11.3 67.9 %all_gather.19 = bf16[2048,16]{0,1:T(8,128)(2,1)S(1)} all-gather(bf16[256,16]{0,1:T(8,128)(2,1)S(1)} %copy-done.66), channel_id=1, replica_groups=mesh['expert'=4,'fsdp'=8] {'fsdp'}, dimensions={0}, use_global_device_ids=true | all-gather | bytes 73728 | tf_op jit(solution)/shard_map/all_gather | solution.py:70
  80.8 413.0 %all-gather.5.cloned.1.call-done = bf16[2048,6144]{1,0:T(8,128)(2,1)} async-done(((bf16[256,6144]{1,0:T(8,128)(2,1)}), bf16[2048,6144]{1,0:T(8,128)(2,1)}) %all-gather.5.cloned.1.call-update) | async-done | bytes 25165840 | tf_op jit(solution)/shard_map/all_gather | solution.py:68
  493.8 11.7 fusion.38
  505.5 1.9 slice_bitcast_fusion
  507.4 1.4 copy-done.20
  508.8 1.7 copy.226
  510.5 1.9 copy.188
  512.5 3.6 multiply_reduce_fusion.9
  517.1 3.3 copy.225
  520.4 3.1 copy.186
  523.5 2.9 multiply_reduce_fusion.10
  527.4 2.2 multiply_multiply_fusion
  535.3 2.1 convolution_convert_fusion.9
  537.4 83.4 %all-gather.7.cloned.1.call-done = bf16[2048,2048]{1,0:T(8,128)(2,1)} async-done(((bf16[256,2048]{1,0:T(8,128)(2,1)}), bf16[2048,2048]{1,0:T(8,128)(2,1)}) %all-gather.7.cloned.1.call-update) | async-done | bytes 8388624 | tf_op jit(solution)/shard_map/all_gather | solution.py:69
  620.8 5.8 multiply_reduce_fusion.8
  629.6 22.2 scatter_custom_fusion.1
  651.8 7.0 all-to-all-start.2
  659.5 21.2 scatter_custom_fusion
  680.7 161.2 %all-to-all-done.2 = bf16[16,256,2048]{2,1,0:T(8,128)(2,1)} async-done(((bf16[16,256,2048]{2,1,0:T(8,128)(2,1)}), bf16[16,256,2048]{2,1,0:T(8,128)(2,1)}, u32[]{:S(2)}, u32[]{:S(2)}) %all-to-all-start.2) | async-done | bytes 16777248 | tf_op jit(solution)/shard_map/all_to_all | solution.py:146
  841.9 7.3 all-to-all-start
  849.3 14.2 copy.199
  863.5 168.8 %all-to-all-done = bf16[16,256,2048]{2,1,0:T(8,128)(2,1)} async-done(((bf16[16,256,2048]{2,1,0:T(8,128)(2,1)}), bf16[16,256,2048]{2,1,0:T(8,128)(2,1)}, u32[]{:S(2)}, u32[]{:S(2)}) %all-to-all-start) | async-done | bytes 16777248 | tf_op jit(solution)/shard_map/all_to_all | solution.py:109
  1032.3 14.2 copy.195
  1046.6 211.8 %all-gather.9.cloned.1.call-done = bf16[4,2048,2048]{2,1,0:T(8,128)(2,1)} async-done(((bf16[4,256,2048]{2,1,0:T(8,128)(2,1)}), bf16[4,2048,2048]{2,1,0:T(8,128)(2,1)}) %all-gather.9.cloned.1.call-update) | async-done | bytes 33554448 | tf_op jit(solution)/shard_map/all_gather | solution.py:117
  1258.3 43.2 %fusion.53 = f32[4,1024,2048]{2,1,0:T(8,128)} fusion(bf16[4,1024,2048]{2,1,0:T(8,128)(2,1)} %bitcast.118, bf16[4,2048,2048]{2,1,0:T(8,128)(2,1)} %all-gather.9.cloned.1.call-done), kind=kOutput, calls=%fused_computation.138 | convolution fusion | flops 34359738368 | bytes 83886080 | tf_op jit(solution)/shard_map/erd,edf->erf/dot_general | solution.py:120
  1301.5 186.5 %all-gather.11.cloned.1.call-done = bf16[4,1024,2048]{2,1,0:T(8,128)(2,1)} async-done(((bf16[4,128,2048]{2,1,0:T(8,128)(2,1)}), bf16[4,1024,2048]{2,1,0:T(8,128)(2,1)}) %all-gather.11.cloned.1.call-update) | async-done | bytes 16777232 | tf_op jit(solution)/shard_map/all_gather | solution.py:118
  1488.0 37.0 %multiply_convert_fusion.1 = (bf16[4,1024,1024]{2,1,0:T(8,128)(2,1)}, bf16[4,1024,1024]{2,1,0:T(8,128)(2,1)}, bf16[4,1024,1024]{2,1,0:T(8,128)(2,1)}) fusion(f32[4,1024,2048]{2,1,0:T(8,128)} %fusion.53, bf16[4,1024,2048]{2,1,0:T(8,128)(2,1)} %bitcast.120, bf16[4,1024,2048]{2,1,0:T(8,128)(2,1)} %all-gather.11.cloned.1.call-done), kind=kOutput, calls=%fused_computation.15 | convolution fusion | flops 17246978048 | bytes 92274688 | tf_op jit(solution)/shard_map/erd,efd->erf/dot_general | solution.py:157
  1525.0 27.3 convolution_convert_fusion.4
  1552.3 22.1 copy.196
  1574.4 7.1 all-to-all-start.1
  1581.5 43.4 %convolution_convert_fusion.2 = bf16[4,1024,2048]{2,1,0:T(8,128)(2,1)} fusion(bf16[4,2048,2048]{2,1,0:T(8,128)(2,1)} %all-gather.9.cloned.1.call-done, bf16[4,1024,1024]{2,1,0:T(8,128)(2,1)} %get-tuple-element.30, bf16[4,1024,1024]{2,1,0:T(8,128)(2,1)} %get-tuple-element.29), kind=kOutput, calls=%fused_computation.18 | convolution fusion | flops 34401681408 | bytes 67108864 | tf_op jit(solution)/shard_map/erf,edf->erd/dot_general | solution.py:169
  1624.9 22.1 copy.202
  1647.0 117.5 %all-to-all-done.1 = bf16[4,1024,2048]{2,0,1:T(4,128)(2,1)} async-done(((bf16[4,1024,2048]{2,0,1:T(4,128)(2,1)}), bf16[4,1024,2048]{2,0,1:T(4,128)(2,1)}, u32[]{:S(2)}, u32[]{:S(2)}) %all-to-all-start.1) | async-done | bytes 16777248 | tf_op jit(solution)/shard_map/all_to_all | solution.py:130
  1764.5 7.4 all-to-all-start.3
  1772.0 18.6 copy.197
  1790.6 24.4 gather_fusion
  1815.1 9.5 fusion.1
  1824.7 130.2 %all-to-all-done.3 = bf16[4,1024,2048]{2,0,1:T(4,128)(2,1)} async-done(((bf16[4,1024,2048]{2,0,1:T(4,128)(2,1)}), bf16[4,1024,2048]{2,0,1:T(4,128)(2,1)}, u32[]{:S(2)}, u32[]{:S(2)}) %all-to-all-start.3) | async-done | bytes 16777248 | tf_op jit(solution)/shard_map/all_to_all | solution.py:172
  1955.0 18.6 copy.203
  1973.6 24.4 gather_fusion.1
  1998.0 11.4 convert_reduce_fusion
  2009.5 3.1 multiply_reduce_fusion.2
  2012.6 1.8 multiply_add_fusion
  2015.7 5.6 convolution_convert_fusion.5
  2022.9 6.1 convolution_convert_fusion.6
  2029.6 4.1 multiply_reduce_fusion
  2039.1 3.0 multiply_reduce_fusion.4
  2045.1 14.6 convolution_convert_fusion.1
  2061.9 27.1 convolution_convert_fusion.3
  2089.1 78.6 %reduce-scatter.8.cloned.1.call-done = bf16[256,2048]{1,0:T(8,128)(2,1)} async-done(((bf16[2048,2048]{1,0:T(8,128)(2,1)}), bf16[256,2048]{1,0:T(8,128)(2,1)}) %reduce-scatter.8.cloned.1.call-update) | async-done | bytes 1048592 | tf_op jit(solution)/shard_map/reduce_scatter | solution.py:245
  2167.7 407.1 %reduce-scatter.6.cloned.1.call-done = bf16[256,6144]{1,0:T(8,128)(2,1)} async-done(((bf16[2048,6144]{1,0:T(8,128)(2,1)}), bf16[256,6144]{1,0:T(8,128)(2,1)}) %reduce-scatter.6.cloned.1.call-update) | async-done | bytes 3145744 | tf_op jit(solution)/shard_map/reduce_scatter | solution.py:242
  2574.9 43.8 %convolution_convert_fusion = bf16[4,2048,2048]{2,1,0:T(8,128)(2,1)} fusion(bf16[4,1024,2048]{2,1,0:T(8,128)(2,1)} %bitcast.119, bf16[4,1024,1024]{2,1,0:T(8,128)(2,1)} %get-tuple-element.30, bf16[4,1024,1024]{2,1,0:T(8,128)(2,1)} %get-tuple-element.29), kind=kOutput, calls=%fused_computation.4 | convolution fusion | flops 34410070016 | bytes 67108864 | tf_op jit(solution)/shard_map/erd,erf->edf/dot_general | solution.py:166
  2618.8 14.2 fusion.22
  2633.0 43.8 %all-reduce = (f32[2048]{0:T(1024)}, f32[128]{0:T(128)}, f32[128]{0:T(128)}, f32[2048]{0:T(1024)}) all-reduce(f32[2048]{0:T(1024)S(1)} %get-tuple-element.19, f32[128]{0:T(128)S(1)} %copy-done.71, f32[128]{0:T(128)S(1)} %copy-done.72, f32[2048]{0:T(1024)S(1)} %copy-done.56), channel_id=1, replica_groups=mesh['expert'=4,'fsdp'=8] {'expert','fsdp'}, use_global_device_ids=true, to_apply=%region_22.0 | all-reduce | flops 4352 | bytes 34816 | tf_op jit(solution)/shard_map/psum | solution.py:257
  2676.8 3.5 fusion.21
  2680.3 6.7 psum.55
  2687.6 230.6 %reduce-scatter.14.cloned.1.call-done = bf16[4,128,2048]{2,1,0:T(8,128)(2,1)} async-done(((bf16[4,1024,2048]{2,1,0:T(8,128)(2,1)}), bf16[4,128,2048]{2,1,0:T(8,128)(2,1)}) %reduce-scatter.14.cloned.1.call-update) | async-done | bytes 2097168 | tf_op jit(solution)/shard_map/reduce_scatter | solution.py:179
  2918.2 4.1 convert_element_type.150
  2922.4 83.0 %all-reduce.4.cloned.1.call-done = (bf16[256,6144]{1,0:T(8,128)(2,1)}, bf16[256,2048]{1,0:T(8,128)(2,1)}) async-done(((bf16[256,6144]{1,0:T(8,128)(2,1)}, bf16[256,2048]{1,0:T(8,128)(2,1)}), (bf16[256,6144]{1,0:T(8,128)(2,1)}, bf16[256,2048]{1,0:T(8,128)(2,1)})) %all-reduce.4.cloned.1.call-update) | async-done | bytes 4194320 | tf_op jit(solution)/shard_map/psum | solution.py:253
  3005.4 2.9 convert_element_type.144
  3008.3 3.4 convert_element_type.142
  3011.8 541.1 %reduce-scatter.12.cloned.1.call-done = bf16[4,256,2048]{2,1,0:T(8,128)(2,1)} async-done(((bf16[4,2048,2048]{2,1,0:T(8,128)(2,1)}), bf16[4,256,2048]{2,1,0:T(8,128)(2,1)}) %reduce-scatter.12.cloned.1.call-update) | async-done | bytes 4194320 | tf_op jit(solution)/shard_map/reduce_scatter | solution.py:176
  3552.9 6.7 convert_element_type.148
  (215 shorter events, 29.8 us)
Async XLA Ops:
  7.2 486.6 %all-gather.5.cloned.1.call-start = ((), (), s32[]{:S(2)}) async-start(), calls=%async_computation.9 | async-start | bytes 28311552 | tf_op jit(solution)/shard_map/all_gather | solution.py:68
  7.2 2.2 copy-start.54
  7.2 2.2 copy-start.65
  7.2 2.5 copy-start.26
  7.9 3.4 copy-start.66
  7.9 612.9 %all-gather.7.cloned.1.call-start = ((), (), s32[]{:S(2)}) async-start(), calls=%async_computation.10 | async-start | bytes 9437184 | tf_op jit(solution)/shard_map/all_gather | solution.py:69
  8.7 71.8 %copy-start.14 = (bf16[256,2048]{1,0:T(8,128)(2,1)S(1)}, bf16[256,2048]{1,0:T(8,128)(2,1)}, u32[]{:S(2)}) copy-start(bf16[256,2048]{1,0:T(8,128)(2,1)} %param.13) | copy-start | bytes 3145732
  8.7 485.1 %copy-start.34 = (f32[2048]{0:T(1024)S(1)}, f32[2048]{0:T(1024)}, u32[]{:S(2)}) copy-start(f32[2048]{0:T(1024)} %param.16) | copy-start | bytes 24580
  8.7 1249.6 %all-gather.9.cloned.1.call-start = ((), (), s32[]{:S(2)}) async-start(), calls=%async_computation.11 | async-start | bytes 37748736 | tf_op jit(solution)/shard_map/all_gather | solution.py:117
  79.2 549.1 %copy-start.36 = (bf16[2048,16]{0,1:T(8,128)(2,1)}, bf16[2048,16]{0,1:T(8,128)(2,1)S(1)}, u32[]{:S(2)}) copy-start(bf16[2048,16]{0,1:T(8,128)(2,1)S(1)} %all_gather.19) | copy-start | bytes 196612
  80.8 424.7 %copy-start.50 = (f32[256]{0:T(256)}, f32[256]{0:T(256)S(1)}, u32[]{:S(2)}) copy-start(f32[256]{0:T(256)S(1)} %add_rsqrt_fusion.3) | copy-start | bytes 3076
  80.8 578.7 %copy-start.57 = (s32[2048,1]{0,1:T(1,128)}, s32[2048,1]{0,1:T(1,128)S(1)}, u32[]{:S(2)}) copy-start(s32[2048,1]{0,1:T(1,128)S(1)} %compare_select_fusion) | copy-start | bytes 24580
  505.5 3.3 copy-start.20
  512.5 14.9 copy-start.4
  520.4 7.0 copy-start.67
  520.4 7.0 copy-start.69
  527.3 2.3 copy-start.44
  527.4 2.2 copy-start.46
  537.4 83.5 %copy-start.18 = (bf16[16,128,256]{2,1,0:T(8,128)(2,1)}, bf16[16,128,256]{2,1,0:T(8,128)(2,1)S(1)}, u32[]{:S(2)}) copy-start(bf16[16,128,256]{2,1,0:T(8,128)(2,1)S(1)} %convolution_convert_fusion.9) | copy-start | bytes 3145732
  620.8 7.2 copy-start.52
  626.7 2.9 copy-start.10
  626.7 25.1 copy-start.61
  628.3 31.2 copy-start.16
  629.3 22.5 copy-start.63
  629.5 22.4 copy-start.32
  651.8 190.1 %all-to-all-start.2 = ((bf16[16,256,2048]{2,1,0:T(8,128)(2,1)}), bf16[16,256,2048]{2,1,0:T(8,128)(2,1)}, u32[]{:S(2)}, u32[]{:S(2)}) async-start(bf16[16,256,2048]{2,1,0:T(8,128)(2,1)} %bitcast.113), calls=%async_computation.2 | async-start | bytes 33554432 | tf_op jit(solution)/shard_map/all_to_all | solution.py:146
  658.9 829.1 %all-gather.11.cloned.1.call-start = ((), (), s32[]{:S(2)}) async-start(), calls=%async_computation.12 | async-start | bytes 18874368 | tf_op jit(solution)/shard_map/all_gather | solution.py:118
  841.9 190.4 %all-to-all-start = ((bf16[16,256,2048]{2,1,0:T(8,128)(2,1)}), bf16[16,256,2048]{2,1,0:T(8,128)(2,1)}, u32[]{:S(2)}, u32[]{:S(2)}) async-start(bf16[16,256,2048]{2,1,0:T(8,128)(2,1)} %bitcast.112), calls=%async_computation | async-start | bytes 33554432 | tf_op jit(solution)/shard_map/all_to_all | solution.py:109
  1574.4 190.1 %all-to-all-start.1 = ((bf16[4,1024,2048]{2,0,1:T(4,128)(2,1)}), bf16[4,1024,2048]{2,0,1:T(4,128)(2,1)}, u32[]{:S(2)}, u32[]{:S(2)}) async-start(bf16[4,1024,2048]{2,0,1:T(4,128)(2,1)} %copy.196), calls=%async_computation.1 | async-start | bytes 33554432 | tf_op jit(solution)/shard_map/all_to_all | solution.py:130
  1647.0 125.0 %copy-start.58 = (s32[2048,1]{0,1:T(1,128)S(1)}, s32[2048,1]{0,1:T(1,128)}, u32[]{:S(2)}) copy-start(s32[2048,1]{0,1:T(1,128)} %copy-done.57) | copy-start | bytes 24580
  1764.5 190.5 %all-to-all-start.3 = ((bf16[4,1024,2048]{2,0,1:T(4,128)(2,1)}), bf16[4,1024,2048]{2,0,1:T(4,128)(2,1)}, u32[]{:S(2)}, u32[]{:S(2)}) async-start(bf16[4,1024,2048]{2,0,1:T(4,128)(2,1)} %copy.202), calls=%async_computation.3 | async-start | bytes 33554432 | tf_op jit(solution)/shard_map/all_to_all | solution.py:172
  1771.9 395.8 %reduce-scatter.8.cloned.1.call-start = ((), (), s32[]{:S(2)}) async-start(), calls=%async_computation.14 | async-start | bytes 9437184 | tf_op jit(solution)/shard_map/reduce_scatter | solution.py:245
  1790.6 24.4 copy-start.11
  1790.6 24.4 copy-start.33
  1815.0 9.6 copy-start.41
  1815.0 9.6 copy-start.60
  1815.0 9.6 copy-start.64
  1815.1 9.6 copy-start.55
  1998.0 11.4 copy-start.3
  1998.0 11.4 copy-start.37
  1998.0 11.4 copy-start.53
  1998.0 11.4 copy-start.62
  2009.4 3.1 copy-start.25
  2009.5 3.1 copy-start.27
  2012.6 3.1 copy-start.19
  2021.3 553.5 %reduce-scatter.6.cloned.1.call-start = ((), (), s32[]{:S(2)}) async-start(), calls=%async_computation.13 | async-start | bytes 28311552 | tf_op jit(solution)/shard_map/reduce_scatter | solution.py:242
  2029.6 4.1 copy-start.1
  2036.9 2.2 copy-start.6
  2036.9 2.2 copy-start.38
  2036.9 2.2 copy-start.45
  2036.9 2.2 copy-start.47
  2036.9 2.2 copy-start.68
  2036.9 2.2 copy-start.70
  2039.1 3.0 copy-start.13
  2042.9 2.1 copy-start.15
  2059.8 620.5 %reduce-scatter.10.cloned.1.call-start = ((), (), s32[]{:S(2)}) async-start(), calls=%async_computation.15 | async-start | bytes 73728 | tf_op jit(solution)/shard_map/reduce_scatter | solution.py:248
  2061.9 856.4 %reduce-scatter.14.cloned.1.call-start = ((), (), s32[]{:S(2)}) async-start(), calls=%async_computation.17 | async-start | bytes 18874368 | tf_op jit(solution)/shard_map/reduce_scatter | solution.py:179
  2089.0 916.3 %all-reduce.4.cloned.1.call-start = ((), (), s32[]{:S(2)}) async-start(), calls=%async_computation.18 | async-start | bytes 8388608 | tf_op jit(solution)/shard_map/psum | solution.py:253
  2574.8 978.0 %reduce-scatter.12.cloned.1.call-start = ((), (), s32[]{:S(2)}) async-start(), calls=%async_computation.16 | async-start | bytes 37748736 | tf_op jit(solution)/shard_map/reduce_scatter | solution.py:176
  2618.7 14.3 copy-start.56
  2618.8 14.3 copy-start.71
  2618.8 14.3 copy-start.72
  2618.8 58.0 %copy-start.9 = (f32[256,2048]{1,0:T(8,128)S(1)}, f32[256,2048]{1,0:T(8,128)}, u32[]{:S(2)}) copy-start(f32[256,2048]{1,0:T(8,128)} %copy-done.7) | copy-start | bytes 6291460
  3005.4 2.9 copy-start.31
  (23 other events, 30.5 us)
Sparse Core Ops, SparseCore 0:
  9.5 484.1 all-gather.4
  495.9 124.9 all-gather.6
  622.4 635.9 all-gather.8
  1260.4 227.5 all-gather.10
  2021.4 146.2 reduce-scatter.7
  2172.0 402.8 reduce-scatter.5
  2578.2 52.8 reduce-scatter.9
  2635.4 282.8 reduce-scatter.13
  2920.7 84.6 all-reduce.3
  3009.5 543.3 reduce-scatter.11
where the time goes:
time: 3570 us
  waiting for transfers between devices  2820 us (79%)
  matrix products  294 us (8%)
  local copies, waits for them, and re-layouts  207 us (6%)
  blocking collectives  118 us (3%)
  other arithmetic  87.1 us (2%)
    reduce_scatter x1, waiting for transfers between devices, local(): lax.psum_scatter(gate_up_grad_full.astype(jnp.bfloat16), 'fsdp', scatter_...  541 us
    all_gather x1, waiting for transfers between devices, local(): lax.all_gather(qkv_weight, 'fsdp', axis=0, tiled=True)  413 us
    reduce_scatter x1, waiting for transfers between devices, local(): lax.psum_scatter(qkv_grad_full.astype(jnp.bfloat16), 'fsdp', scatter_dime...  407 us
    reduce_scatter x1, waiting for transfers between devices, local(): lax.psum_scatter(down_grad_full.astype(jnp.bfloat16), 'fsdp', scatter_dim...  231 us
    all_gather x1, waiting for transfers between devices, local(): lax.all_gather(gate_up_weight, 'fsdp', axis=1, tiled=True)  212 us
    all_gather x1, waiting for transfers between devices, local(): lax.all_gather(down_weight, 'fsdp', axis=1, tiled=True)  187 us
    all_to_all x1, waiting for transfers between devices, local(): lax.all_to_all(outgoing.reshape(experts, capacity, model_width), 'expert'...  169 us
    all_to_all x1, waiting for transfers between devices, local(): lax.all_to_all(grad_out.reshape(experts, capacity, model_width), 'expert'...  161 us
  transfers between devices with their start and end apart: 14, of which 13 were waited for; matrix products, arithmetic and copies ran while one was open for 12% of the time, Pallas kernels for 0%

commit v1 on v0

v1 whole, which is shorter than its diff:
```python
import math

import jax
import jax.numpy as jnp
from jax import lax
from jax.sharding import Mesh, PartitionSpec as P

EPSILON = 1e-06
ROPE_BASE = 50000.0
F32 = jnp.float32
BF16 = jnp.bfloat16
LANES = 128


def dot(left, right, out=F32):
    return jnp.dot(left, right, preferred_element_type=F32).astype(out)


def dot_nt(left, right, out=F32):
    return lax.dot_general(
        left, right, (((1,), (1,)), ((), ())), preferred_element_type=F32
    ).astype(out)


def dot_tn(left, right, out=F32):
    return lax.dot_general(
        left, right, (((0,), (0,)), ((), ())), preferred_element_type=F32
    ).astype(out)


def normalize(values):
    factor = lax.rsqrt(jnp.mean(values * values, -1, keepdims=True) + EPSILON)
    return (values * factor, factor)


def norm_back(grad_unit, unit_val, factor):
    return factor * (grad_unit - unit_val * jnp.mean(grad_unit * unit_val, -1, keepdims=True))


def tables(length, head_size):
    half_size = head_size // 2
    frequency = ROPE_BASE ** (-(jnp.arange(half_size, dtype=F32) * 2.0 / head_size))
    angles = jnp.arange(length, dtype=F32)[:, None] * frequency[None, :]
    angles = jnp.concatenate([angles, angles], 1)
    return (jnp.cos(angles)[:, None, :], jnp.sin(angles)[:, None, :])


def rotate(values, cos_table, sine_table):
    half_size = values.shape[-1] // 2
    turned = jnp.concatenate([-values[..., half_size:], values[..., :half_size]], -1)
    return values * cos_table + turned * sine_table


def rotate_back(gradient, cos_table, sine_table):
    half_size = gradient.shape[-1] // 2
    turned_grad = gradient * sine_table
    return gradient * cos_table + jnp.concatenate(
        [turned_grad[..., half_size:], -turned_grad[..., :half_size]], -1
    )


def take(array, index):
    return lax.dynamic_index_in_dim(array, index, 0, keepdims=False)


def put(array, part, index):
    return lax.dynamic_update_index_in_dim(array, part, index, 0)


def shift(value, axis, size, step):
    return lax.ppermute(value, axis, [(i, (i + step) % size) for i in range(size)])


def exchange(blocks, axis, size):
    me = lax.axis_index(axis)
    result = put(jnp.zeros_like(blocks), take(blocks, me), me)
    for step in range(1, size):
        moved = shift(take(blocks, (me + step) % size), axis, size, step)
        result = put(result, moved, (me - step) % size)
    return result


def gather_square(own):
    my_y, my_b = lax.axis_index("y"), lax.axis_index("b")
    half = own.shape[0] // 2
    over_b = shift(own, "b", 2, 1)
    over_y = shift(own, "y", 2, 1)
    far = jnp.concatenate([shift(over_y[:half], "b", 2, 1), shift(over_b[half:], "y", 2, 1)], 0)
    same_y = jnp.where(my_b == 0, jnp.stack([own, over_b]), jnp.stack([over_b, own]))
    other_y = jnp.where(my_b == 0, jnp.stack([over_y, far]), jnp.stack([far, over_y]))
    return same_y, other_y


def add(left, right):
    return (left.astype(F32) + right.astype(F32)).astype(BF16)


def scatter_square(same_y, other_y):
    my_b = lax.axis_index("b")
    half = same_y.shape[1] // 2
    far = take(other_y, 1 - my_b)
    for_y = take(other_y, my_b)
    for_b = take(same_y, 1 - my_b)
    got_b = shift(far[:half], "b", 2, 1)
    got_y = shift(far[half:], "y", 2, 1)
    for_y = jnp.concatenate([add(for_y[:half], got_b), for_y[half:]], 0)
    for_b = jnp.concatenate([for_b[:half], add(for_b[half:], got_y)], 0)
    got_y = shift(for_y, "y", 2, 1)
    got_b = shift(for_b, "b", 2, 1)
    return (take(same_y, my_b).astype(F32) + got_y.astype(F32) + got_b.astype(F32)).astype(BF16)


def build(y_size, c_size, a_size, b_size):
    square = y_size == 2 and b_size == 2
    everywhere = ("a", "b", "y", "c")

    def reduce_rows(left, right):
        tokens, width = left.shape
        columns = right.shape[1]
        left = left.reshape(tokens, a_size, b_size, y_size, c_size, -1)
        piece = left.shape[-1]
        left = left.transpose(4, 0, 3, 2, 1, 5).reshape(c_size, tokens, width // c_size)
        my_c, my_y = lax.axis_index("c"), lax.axis_index("y")
        other = dot_tn(take(left, 1 - my_c), right, BF16)
        got = shift(other, "c", c_size, 1)
        mine = dot_tn(take(left, my_c), right)
        mine = (mine + got.astype(F32)).astype(BF16)
        mine = mine.reshape(y_size, b_size, a_size * piece, columns)
        if square:
            mine = scatter_square(take(mine, my_y), take(mine, 1 - my_y))
        else:
            mine = mine.reshape(y_size * b_size * a_size * piece, columns)
            mine = lax.psum_scatter(mine, ("y", "b"), scatter_dimension=0, tiled=True)
        mine = lax.psum_scatter(mine, "a", scatter_dimension=0, tiled=True)
        return lax.all_gather(mine, ("y", "c"), axis=0, tiled=True)

    def local(
        layer_input,
        expert_ids,
        slot_ids,
        attn_gain,
        qkv_weight,
        query_gain,
        key_gain,
        out_weight,
        ffn_gain,
        router_weight,
        gate_up_weight,
        down_weight,
        cotangent,
    ):
        tokens, model_width = layer_input.shape
        head_size = query_gain.shape[0]
        head_count = model_width // head_size
        experts = router_weight.shape[1]
        held, d_block, both = gate_up_weight.shape
        hidden = both // 2
        f_block = down_weight.shape[1]
        share = held // a_size
        score_scale = head_size ** (-0.5)
        my_y, my_c = lax.axis_index("y"), lax.axis_index("c")
        my_a, my_b = lax.axis_index("a"), lax.axis_index("b")

        part = qkv_weight.shape[0] // (y_size * c_size)
        spot = (my_y * c_size + my_c) * part
        qkv_full = lax.all_gather(
            lax.dynamic_slice_in_dim(qkv_weight, spot, part, 0), everywhere, axis=0, tiled=True
        )
        out_full = lax.all_gather(
            lax.dynamic_slice_in_dim(out_weight, spot, part, 0), everywhere, axis=0, tiled=True
        )
        router_full = lax.all_gather(router_weight, ("a", "b"), axis=0, tiled=True)

        def reorder(values):
            shape = values.shape[:-1]
            values = values.reshape(*shape, 2, a_size, b_size, f_block)
            return values.swapaxes(-3, -2).reshape(*shape, both)

        gate_up_sent = exchange(
            reorder(gate_up_weight).reshape(a_size, share, d_block, both), "a", a_size
        ).transpose(1, 0, 2, 3)
        down_sent = exchange(
            down_weight.reshape(a_size, share, f_block, model_width), "a", a_size
        ).transpose(1, 0, 2, 3)
        gate_up_sent = gate_up_sent.reshape(share * a_size * d_block, both)
        down_sent = down_sent.reshape(share * a_size * f_block, model_width)
        if square:
            gate_up_list = [
                half.reshape(b_size, share, a_size * d_block, both)
                for half in gather_square(gate_up_sent)
            ]
            down_list = [
                half.reshape(b_size, share, a_size * f_block, model_width)
                for half in gather_square(down_sent)
            ]
            owners = [my_y, 1 - my_y]
        else:
            gate_up_all = lax.all_gather(gate_up_sent, ("y", "b"), axis=0, tiled=True)
            down_all = lax.all_gather(down_sent, ("y", "b"), axis=0, tiled=True)
            gate_up_all = gate_up_all.reshape(y_size, b_size, share, a_size * d_block, both)
            down_all = down_all.reshape(y_size, b_size, share, a_size * f_block, model_width)
            gate_up_list = [gate_up_all[i] for i in range(y_size)]
            down_list = [down_all[i] for i in range(y_size)]
            owners = list(range(y_size))
        weights = []
        for owner, gate_up_part, down_part in zip(owners, gate_up_list, down_list):
            for s in range(share):
                number = ((owner * c_size + my_c) * a_size + my_a) * share + s
                weights.append(
                    (
                        number,
                        gate_up_part[:, s].reshape(model_width, both),
                        down_part[:, s].reshape(hidden, model_width),
                    )
                )

        upstream_all = lax.all_gather(cotangent, ("a", "c"), axis=0, tiled=True)

        source = layer_input.astype(F32)
        unit_one, factor_one = normalize(source)
        normed = (unit_one * attn_gain).astype(BF16)
        projected = dot(normed, qkv_full)
        queries = projected[:, :model_width].reshape(tokens, head_count, head_size)
        keys_raw = projected[:, model_width : 2 * model_width].reshape(
            tokens, head_count, head_size
        )
        values_raw = projected[:, 2 * model_width :].reshape(tokens, head_count, head_size)
        unit_query, factor_query = normalize(queries)
        unit_key, factor_key = normalize(keys_raw)
        cos_table, sine_table = tables(tokens, head_size)
        query_rot = rotate(unit_query * query_gain, cos_table, sine_table).astype(BF16)
        key_rot = rotate(unit_key * key_gain, cos_table, sine_table).astype(BF16)
        value_low = values_raw.astype(BF16)
        scores = (
            jnp.einsum("qhd,khd->hqk", query_rot, key_rot, preferred_element_type=F32)
            * score_scale
        )
        top_score = jnp.max(scores, -1, keepdims=True)
        weights_raw = jnp.exp(scores - top_score)
        totals = jnp.sum(weights_raw, -1, keepdims=True)
        prob_full = weights_raw / totals
        prob_low = prob_full.astype(BF16)
        mixed_heads = jnp.einsum("hqk,khd->qhd", prob_low, value_low, preferred_element_type=F32)
        mixed_low = mixed_heads.reshape(tokens, model_width).astype(BF16)
        residual = source + dot(mixed_low, out_full)
        unit_two, factor_two = normalize(residual)
        normed_two = (unit_two * ffn_gain).astype(BF16)
        logits = dot(normed_two, router_full)
        onehot = (
            expert_ids[:, :, None] == jnp.arange(experts, dtype=jnp.int32)[None, None, :]
        ).astype(F32)
        chosen = jnp.sum(onehot * logits[:, None, :], -1)
        gate_probs = jax.nn.softmax(chosen, -1)
        gate_dense = jnp.sum(onehot * gate_probs[:, :, None], 1)

        def swap_blocks(values, first, second):
            rows = values.shape[0]
            values = values.reshape(rows, first, second, d_block)
            return values.transpose(0, 2, 1, 3).reshape(rows, model_width)

        def split(values):
            high = values.astype(BF16)
            low = (values - high.astype(F32)).astype(BF16)
            pad = jnp.zeros((values.shape[0], LANES - 2 * experts), BF16)
            return jnp.concatenate([high, low, pad], 1)

        def join(values):
            return values[:, :experts].astype(F32) + values[:, experts : 2 * experts].astype(F32)

        rows_sent = jnp.concatenate(
            [swap_blocks(normed_two, a_size, b_size), split(gate_dense)], 1
        )
        rows_all = lax.all_gather(rows_sent, ("a", "c"), axis=0, tiled=True)
        rows_in = rows_all[:, :model_width]
        gates_all = join(rows_all[:, model_width:])
        numbers = jnp.arange(experts, dtype=jnp.int32)[None, :]
        moe_part = 0.0
        row_part = 0.0
        gate_grad_part = jnp.zeros((rows_all.shape[0], experts), F32)
        grads = []
        for number, gate_up_full, down_full in weights:
            mask = (numbers == number).astype(F32)
            gate_here = jnp.sum(gates_all * mask, 1, keepdims=True)
            gate_up_val = dot(rows_in, gate_up_full)
            gate_part = gate_up_val[:, :hidden]
            up_part = gate_up_val[:, hidden:]
            sigmoid_gate = jax.nn.sigmoid(gate_part)
            activated = gate_part * sigmoid_gate * up_part
            act_grad = dot_nt(upstream_all, down_full)
            gate_grad_part = gate_grad_part + mask * jnp.sum(
                activated * act_grad, -1, keepdims=True
            )
            act_gated = (gate_here * activated).astype(BF16)
            act_grad = gate_here * act_grad
            gate_side = act_grad * up_part * sigmoid_gate * (1.0 + gate_part * (1.0 - sigmoid_gate))
            up_side = act_grad * gate_part * sigmoid_gate
            both_grad = jnp.concatenate([gate_side, up_side], -1).astype(BF16)
            row_part = row_part + dot_nt(both_grad, gate_up_full)
            moe_part = moe_part + dot(act_gated, down_full)
            grads.append(
                (dot_tn(rows_in, both_grad, BF16), dot_tn(act_gated, upstream_all, BF16))
            )
        back_sent = jnp.concatenate([row_part.astype(BF16), split(gate_grad_part)], 1)
        back = lax.psum_scatter(back_sent, ("a", "c"), scatter_dimension=0, tiled=True)
        moe_sum = lax.psum_scatter(
            moe_part.astype(BF16), ("a", "c"), scatter_dimension=0, tiled=True
        )
        mixed_out = (residual + moe_sum.astype(F32)).astype(BF16)

        def home(parts, block):
            columns = parts[0].shape[1]
            parts = [
                jnp.stack(parts[i * share : (i + 1) * share]).reshape(
                    share, b_size, a_size * block, columns
                )
                for i in range(y_size)
            ]
            parts = [p.swapaxes(0, 1).reshape(b_size, share * a_size * block, columns) for p in parts]
            if square:
                summed = scatter_square(parts[0], parts[1])
            else:
                summed = lax.psum_scatter(
                    jnp.stack(parts).reshape(-1, columns),
                    ("y", "b"),
                    scatter_dimension=0,
                    tiled=True,
                )
            summed = summed.reshape(share, a_size, block, columns).swapaxes(0, 1)
            return exchange(summed, "a", a_size).reshape(held, block, columns)

        gate_up_grad = home([g[0] for g in grads], d_block)
        down_grad = home([g[1] for g in grads], f_block).astype(F32)
        gate_up_grad = gate_up_grad.reshape(held, d_block, 2, b_size, a_size, f_block)
        gate_up_grad = gate_up_grad.swapaxes(3, 4).reshape(held, d_block, both).astype(F32)

        upstream = cotangent.astype(F32)
        gate_grad = join(back[:, model_width:])
        mean_grad = jnp.sum(gate_dense * gate_grad, -1, keepdims=True)
        logit_grad = (gate_dense * (gate_grad - mean_grad)).astype(BF16)
        normed_two_grad = swap_blocks(back[:, :model_width], b_size, a_size).astype(
            F32
        ) + dot_nt(logit_grad, router_full)
        ffn_gain_part = jnp.sum(normed_two_grad * unit_two, 0)
        residual_grad = upstream + norm_back(normed_two_grad * ffn_gain, unit_two, factor_two)
        attn_grad_low = residual_grad.astype(BF16)
        router_grad_full = dot_tn(normed_two, logit_grad, BF16)
        router_shard = lax.psum_scatter(
            router_grad_full, ("a", "b"), scatter_dimension=0, tiled=True
        )
        router_weight_grad = lax.psum(router_shard, ("y", "c")).astype(F32)
        out_weight_grad = reduce_rows(mixed_low, attn_grad_low).astype(F32)
        mixed_grad = dot_nt(attn_grad_low, out_full, BF16)
        mixed_grad = mixed_grad.reshape(tokens, head_count, head_size)
        value_grad = jnp.einsum("hqk,qhd->khd", prob_low, mixed_grad, preferred_element_type=F32)
        prob_grad = jnp.einsum("qhd,khd->hqk", mixed_grad, value_low, preferred_element_type=F32)
        score_grad = (
            prob_full * (prob_grad - jnp.sum(prob_full * prob_grad, -1, keepdims=True))
        ).astype(BF16)
        query_grad = (
            jnp.einsum("hqk,khd->qhd", score_grad, key_rot, preferred_element_type=F32)
            * score_scale
        )
        key_grad = (
            jnp.einsum("hqk,qhd->khd", score_grad, query_rot, preferred_element_type=F32)
            * score_scale
        )
        query_grad = rotate_back(query_grad, cos_table, sine_table)
        key_grad = rotate_back(key_grad, cos_table, sine_table)
        query_gain_part = jnp.sum(query_grad * unit_query, (0, 1))
        key_gain_part = jnp.sum(key_grad * unit_key, (0, 1))
        query_pre = norm_back(query_grad * query_gain, unit_query, factor_query)
        key_pre = norm_back(key_grad * key_gain, unit_key, factor_key)
        qkv_grad_low = jnp.concatenate(
            [
                query_pre.reshape(tokens, model_width),
                key_pre.reshape(tokens, model_width),
                value_grad.reshape(tokens, model_width),
            ],
            1,
        ).astype(BF16)
        qkv_weight_grad = reduce_rows(normed, qkv_grad_low).astype(F32)
        normed_grad = dot_nt(qkv_grad_low, qkv_full)
        attn_gain_part = jnp.sum(normed_grad * unit_one, 0)
        input_grad = residual_grad + norm_back(normed_grad * attn_gain, unit_one, factor_one)
        gains = jnp.concatenate([attn_gain_part, ffn_gain_part, query_gain_part, key_gain_part])
        gains = jnp.sum(lax.all_gather(gains[None], everywhere, axis=0, tiled=True), 0)
        attn_gain_grad = gains[:model_width]
        ffn_gain_grad = gains[model_width : 2 * model_width]
        query_gain_grad = gains[2 * model_width : 2 * model_width + head_size]
        key_gain_grad = gains[2 * model_width + head_size :]
        return (
            mixed_out,
            input_grad,
            attn_gain_grad,
            qkv_weight_grad,
            query_gain_grad,
            key_gain_grad,
            out_weight_grad,
            ffn_gain_grad,
            router_weight_grad,
            gate_up_grad,
            down_grad,
        )

    return local


def solution(mesh):
    c_size, a_size = 2, 4
    y_size = mesh.shape["expert"] // c_size
    b_size = mesh.shape["fsdp"] // a_size
    fine = Mesh(mesh.devices.reshape(y_size, c_size, a_size, b_size), ("y", "c", "a", "b"))
    rows, model, held = P(("y", "c", "a", "b"), None), P(("a", "b"), None), P(("y", "c"), ("a", "b"), None)
    return jax.shard_map(
        build(y_size, c_size, a_size, b_size),
        mesh=fine,
        in_specs=(rows, rows, rows, P(), model, P(), P(), model, P(), model, held, held, rows),
        out_specs=(rows, rows, P(), model, P(), P(), model, P(), model, held, held),
        check_vma=False,
    )
```

time: 3570 us -> 1740 us (0.49)
  waiting for transfers between devices: 2820 us -> 920 us
  starting transfers between devices: 30.1 us -> 97.2 us
  local copies, waits for them, and re-layouts: 207 us -> 142 us
  matrix products: 294 us -> 336 us
  other arithmetic: 87.1 us -> 129 us
    reduce_scatter x5, waiting for transfers between devices: 1260 us -> 192 us  [the longest x1 114 us: local(): lax.psum_scatter(back_sent, ('a', 'c'), scatter_dimension=0, tiled=True)]
    all_gather x4 -> x6, waiting for transfers between devices: 895 us -> 157 us  [the longest x1 120 us: local(): lax.all_gather(lax.dynamic_slice_in_dim(qkv_weight, spot, part, 0), every...]
    all_to_all x4 -> x0, waiting for transfers between devices: 578 us -> none  [the longest x1 169 us: local(): lax.all_to_all(outgoing.reshape(experts, capacity, model_width), 'expert'...]
    ppermute x0 -> x38, waiting for transfers between devices: none -> 571 us  [shift(): lax.ppermute(value, axis, [(i, (i + step) % size) for i in range(size)])]
    ppermute x0 -> x38, starting transfers between devices: none -> 96.5 us  [shift(): lax.ppermute(value, axis, [(i, (i + step) % size) for i in range(size)])]
    psum x1 -> x0, waiting for transfers between devices: 83 us -> none  [local(): lax.psum(qkv_shard.astype(jnp.bfloat16), 'expert').astype(jnp.float32)]
    all_to_all x4 -> x0, local copies, waits for them, and re-layouts: 65.7 us -> none  [the longest x1 18.6 us: local(): lax.all_to_all(expert_out, 'expert', split_axis=1, concat_axis=0, tiled=T...]
    gather x2 -> x0, local copies, waits for them, and re-layouts: 48.8 us -> none  [the longest x1 24.4 us: local(): rows_back[slot_index].reshape(tokens, top_count, model_width)]
  transfers between devices with their start and end apart: 14 -> 49, of which waited for: 13 -> 24; matrix products, arithmetic and copies ran while one was open for 12% -> 25% of each run, Pallas kernels for 0% -> 0%
where the time goes in v1:
time: 1740 us; the launch traced here: 1730 us
  waiting for transfers between devices  920 us (53%)
  matrix products  336 us (19%)
  local copies, waits for them, and re-layouts  142 us (8%)
  other arithmetic  129 us (7%)
  starting transfers between devices  97.2 us (6%)
  blocking collectives  86.9 us (5%)
    ppermute x38, waiting for transfers between devices, shift(): lax.ppermute(value, axis, [(i, (i + step) % size) for i in range(size)])  571 us
    dot_general x7, matrix products, dot_nt(): lax.dot_general(left, right, (((1,), (1,)), ((), ())), preferred_element_...  121 us
    all_gather x1, waiting for transfers between devices, local(): lax.all_gather(lax.dynamic_slice_in_dim(qkv_weight, spot, part, 0), every...  120 us
    reduce_scatter x1, waiting for transfers between devices, local(): lax.psum_scatter(back_sent, ('a', 'c'), scatter_dimension=0, tiled=True)  114 us
    dot_general x9, matrix products, dot_tn(): lax.dot_general(left, right, (((0,), (0,)), ((), ())), preferred_element_...  99.9 us
    dot_general x7, matrix products, dot(): return jnp.dot(left, right, preferred_element_type=F32).astype(out)  99.4 us
    ppermute x38, starting transfers between devices, shift(): lax.ppermute(value, axis, [(i, (i + step) % size) for i in range(size)])  96.5 us
    reduce_scatter x1, waiting for transfers between devices, local(): lax.psum_scatter(moe_part.astype(BF16), ('a', 'c'), scatter_dimension=0,...  78 us
  transfers between devices with their start and end apart: 49, of which 24 were waited for; matrix products, arithmetic and copies ran while one was open for 25% of the time, Pallas kernels for 0%

profile of v1, /device:TPU:0, one launch (start us, length us, event | category | flops | bytes accessed | tf_op | source)
XLA Modules:
  0.0 1726.7 jit_solution(9134577577370775420)
XLA Ops:
  11.9 32.8 %all_gather.26 = bf16[2048,16]{0,1:T(8,128)(2,1)S(1)} all-gather(bf16[256,16]{0,1:T(8,128)(2,1)} %param.21), channel_id=1, replica_groups=mesh['y'=2,'c'=2,'a'=4,'b'=2] {'a','b'}, dimensions={0}, use_global_device_ids=true | all-gather | bytes 73728 | tf_op jit(solution)/shard_map/all_gather | solution.py:172
  49.1 120.1 %all-gather.9.cloned.1.call-done = bf16[2048,6144]{1,0:T(8,128)(2,1)} async-done(((bf16[64,6144]{1,0:T(8,128)(2,1)}), bf16[2048,6144]{1,0:T(8,128)(2,1)}) %all-gather.9.cloned.1.call-update) | async-done | bytes 25165840 | tf_op jit(solution)/shard_map/all_gather | solution.py:166
  169.2 11.6 fusion.93
  206.7 4.5 convolution_convert_fusion.9
  211.2 36.9 %all-gather.11.cloned.1.call-done = bf16[2048,2048]{1,0:T(8,128)(2,1)} async-done(((bf16[64,2048]{1,0:T(8,128)(2,1)}), bf16[2048,2048]{1,0:T(8,128)(2,1)}) %all-gather.11.cloned.1.call-update) | async-done | bytes 8388624 | tf_op jit(solution)/shard_map/all_gather | solution.py:169
  248.1 6.2 multiply_reduce_fusion.8
  257.7 3.6 copy.259
  264.0 6.2 copy.260
  270.3 5.3 copy.261
  297.5 34.4 %collective-permute-done = bf16[1,256,2048]{2,1,0:T(8,128)(2,1)} collective-permute-done((bf16[1,256,2048]{2,1,0:T(8,128)(2,1)}, bf16[1,256,2048]{2,1,0:T(8,128)(2,1)}, u32[]{:S(2)}, u32[]{:S(2)}) %collective-permute-start) | collective-permute-done | bytes 1048608 | tf_op jit(solution)/shard_map/ppermute | solution.py:71
  331.9 9.6 collective-permute-start.6
  343.8 57.7 %collective-permute-done.1 = bf16[1,256,2048]{2,1,0:T(8,128)(2,1)} collective-permute-done((bf16[1,256,2048]{2,1,0:T(8,128)(2,1)}, bf16[1,256,2048]{2,1,0:T(8,128)(2,1)}, u32[]{:S(2)}, u32[]{:S(2)}) %collective-permute-start.1) | collective-permute-done | bytes 1048608 | tf_op jit(solution)/shard_map/ppermute | solution.py:71
  409.0 17.2 collective-permute-done.4
  427.3 55.3 %collective-permute-done.5 = bf16[1,128,2048]{2,1,0:T(8,128)(2,1)} collective-permute-done((bf16[1,128,2048]{2,1,0:T(8,128)(2,1)}, bf16[1,128,2048]{2,1,0:T(8,128)(2,1)}, u32[]{:S(2)}, u32[]{:S(2)}) %collective-permute-start.5) | collective-permute-done | bytes 524320 | tf_op jit(solution)/shard_map/ppermute | solution.py:71
  486.7 55.7 %collective-permute-done.7 = bf16[512,2048]{1,0:T(8,128)(2,1)S(1)} collective-permute-done((bf16[512,2048]{1,0:T(8,128)(2,1)S(1)}, bf16[512,2048]{1,0:T(8,128)(2,1)S(1)}, u32[]{:S(2)}, u32[]{:S(2)}) %collective-permute-start.7) | collective-permute-done | bytes 2097184 | tf_op jit(solution)/shard_map/ppermute | solution.py:71
  555.7 13.0 collective-permute-done.13
  568.8 4.0 collective-permute-done.12
  576.9 10.6 maximum_select_fusion
  587.5 24.2 %collective-permute-done.10 = bf16[512,2048]{1,0:T(8,128)(2,1)S(1)} collective-permute-done((bf16[512,2048]{1,0:T(8,128)(2,1)S(1)}, bf16[512,2048]{1,0:T(8,128)(2,1)S(1)}, u32[]{:S(2)}, u32[]{:S(2)}) %collective-permute-start.10) | collective-permute-done | bytes 2097184 | tf_op jit(solution)/shard_map/ppermute | solution.py:71
  611.7 3.8 collective-permute-done.9
  616.1 7.9 maximum_select_fusion.1
  625.1 24.6 %fusion.10 = f32[2048,2048]{0,1:T(8,128)} fusion(bf16[2048,2048]{1,0:T(8,128)(2,1)} %bitcast.306, bf16[2048,2176]{0,1:T(8,128)(2,1)} %all-gather.13.cloned.1.call-done), kind=kOutput, calls=%fused_computation.38 | convolution fusion | flops 17179869184 | bytes 33554432 | tf_op jit(solution)/shard_map/dot_general | solution.py:16
  649.7 23.2 %fusion.12 = f32[2048,2048]{0,1:T(8,128)} fusion(bf16[2048,2048]{1,0:T(8,128)(2,1)} %bitcast.304, bf16[2048,2176]{0,1:T(8,128)(2,1)S(1)} %copy-done.81), kind=kOutput, calls=%fused_computation.40 | convolution fusion | flops 17179869184 | bytes 33554432 | tf_op jit(solution)/shard_map/dot_general | solution.py:16
  672.8 23.4 %multiply_convert_fusion.1 = (bf16[2048,1024]{0,1:T(8,128)(2,1)}, bf16[2048,1024]{0,1:T(8,128)(2,1)}, f32[2048]{0:T(1024)S(1)}, f32[2048,1024]{0,1:T(8,128)}) fusion(f32[2048,2048]{0,1:T(8,128)} %fusion.10, f32[2048]{0:T(1024)S(1)} %get-tuple-element.77, bf16[1024,2048]{1,0:T(8,128)(2,1)} %bitcast.324, bf16[2048,2048]{1,0:T(8,128)(2,1)} %all-gather.15.cloned.1.call-done), kind=kOutput, calls=%fused_computation.21 | convolution fusion | flops 8627681280 | bytes 46153728 | tf_op jit(solution)/shard_map/dot_general | solution.py:20
  696.2 23.2 %multiply_convert_fusion.3 = (bf16[2048,1024]{0,1:T(8,128)(2,1)}, bf16[2048,1024]{0,1:T(8,128)(2,1)}, f32[2048]{0:T(1024)S(1)}, f32[2048,1024]{0,1:T(8,128)}) fusion(f32[2048,2048]{0,1:T(8,128)} %fusion.12, f32[2048]{0:T(1024)S(1)} %get-tuple-element.78, bf16[1024,2048]{1,0:T(8,128)(2,1)} %bitcast.322, bf16[2048,2048]{1,0:T(8,128)(2,1)} %all-gather.15.cloned.1.call-done), kind=kOutput, calls=%fused_computation.23 | convolution fusion | flops 8627681280 | bytes 46153728 | tf_op jit(solution)/shard_map/dot_general | solution.py:20
  719.5 24.5 %fusion.7 = f32[2048,2048]{0,1:T(8,128)} fusion(bf16[2048,2048]{1,0:T(8,128)(2,1)} %bitcast.305, bf16[2048,1024]{0,1:T(8,128)(2,1)} %get-tuple-element.98, bf16[2048,1024]{0,1:T(8,128)(2,1)} %get-tuple-element.97), kind=kOutput, calls=%fused_computation.35 | convolution fusion | flops 17196646400 | bytes 33554432 | tf_op jit(solution)/shard_map/dot_general | solution.py:20
  744.0 25.4 %add_convert_fusion.1 = bf16[2048,2048]{0,1:T(8,128)(2,1)} fusion(f32[2048,2048]{0,1:T(8,128)} %fusion.7, bf16[2048,2048]{1,0:T(8,128)(2,1)} %bitcast.307, bf16[2048,1024]{0,1:T(8,128)(2,1)} %get-tuple-element.96, bf16[2048,1024]{0,1:T(8,128)(2,1)} %get-tuple-element.95), kind=kOutput, calls=%fused_computation.2 | convolution fusion | flops 17205035008 | bytes 41943040 | tf_op jit(solution)/shard_map/dot_general | solution.py:20
  769.4 13.3 maximum_maximum_fusion
  782.8 16.4 fusion.43
  799.2 17.2 add_convert_fusion.2
  819.4 114.0 %reduce-scatter.8.cloned.1.call-done = bf16[256,2176]{0,1:T(8,128)(2,1)} async-done(((bf16[2048,2176]{0,1:T(8,128)(2,1)}), bf16[256,2176]{0,1:T(8,128)(2,1)}) %reduce-scatter.8.cloned.1.call-update) | async-done | bytes 1114128 | tf_op jit(solution)/shard_map/reduce_scatter | solution.py:304
  937.1 3.9 reshape.359
  941.8 4.2 multiply_reduce_fusion.4
  946.1 78.0 %reduce-scatter.6.cloned.1.call-done = bf16[256,2048]{1,0:T(8,128)(2,1)} async-done(((bf16[2048,2048]{1,0:T(8,128)(2,1)}), bf16[256,2048]{1,0:T(8,128)(2,1)}) %reduce-scatter.6.cloned.1.call-update) | async-done | bytes 1048592 | tf_op jit(solution)/shard_map/reduce_scatter | solution.py:305
  1028.9 5.8 convolution_convert_fusion.6
  1035.2 4.2 convolution_convert_fusion.8
  1052.2 9.9 convolution_convert_fusion
  1064.1 23.5 %convolution_convert_fusion.1 = bf16[2048,2048]{1,0:T(8,128)(2,1)} fusion(bf16[2048,1024]{0,1:T(8,128)(2,1)} %get-tuple-element.96, bf16[2048,1024]{0,1:T(8,128)(2,1)} %get-tuple-element.95, bf16[2048,2176]{0,1:T(8,128)(2,1)} %all-gather.13.cloned.1.call-done), kind=kOutput, calls=%fused_computation.30 | convolution fusion | flops 17200840704 | bytes 25165824 | tf_op jit(solution)/shard_map/dot_general | solution.py:26
  1087.6 5.8 dynamic-slice_bitcast_fusion.4
  1094.9 23.9 %convolution_convert_fusion.2 = bf16[2048,2048]{1,0:T(8,128)(2,1)} fusion(bf16[2048,1024]{0,1:T(8,128)(2,1)} %get-tuple-element.98, bf16[2048,1024]{0,1:T(8,128)(2,1)} %get-tuple-element.97, bf16[2048,2176]{0,1:T(8,128)(2,1)} %all-gather.13.cloned.1.call-done), kind=kOutput, calls=%fused_computation.31 | convolution fusion | flops 17200840704 | bytes 25165824 | tf_op jit(solution)/shard_map/dot_general | solution.py:26
  1125.5 9.5 add_convert_fusion
  1135.0 3.6 dynamic-slice_bitcast_fusion.10
  1140.7 13.8 convolution_convert_fusion.3
  1159.6 16.4 collective-permute-done.15
  1176.0 11.1 collective-permute-done.17
  1197.1 15.1 convolution_convert_fusion.4
  1221.3 44.7 %collective-permute-done.18 = bf16[256,6144]{1,0:T(8,128)(2,1)} collective-permute-done((bf16[256,6144]{1,0:T(8,128)(2,1)}, bf16[256,6144]{1,0:T(8,128)(2,1)}, u32[]{:S(2)}, u32[]{:S(2)}) %collective-permute-start.18) | collective-permute-done | bytes 3145760 | tf_op jit(solution)/shard_map/ppermute | solution.py:71
  1266.5 10.5 collective-permute-done.16
  1277.1 7.1 fusion.6
  1284.5 14.1 collective-permute-done.33
  1319.1 14.3 collective-permute-done.31
  1337.2 129.1 %collective-permute-done.34 = bf16[512,2048]{1,0:T(8,128)(2,1)S(1)} collective-permute-done((bf16[512,2048]{1,0:T(8,128)(2,1)S(1)}, bf16[512,2048]{1,0:T(8,128)(2,1)S(1)}, u32[]{:S(2)}, u32[]{:S(2)}) %collective-permute-start.34) | collective-permute-done | bytes 2097184 | tf_op jit(solution)/shard_map/ppermute | solution.py:71
  1471.9 10.1 fusion.2
  1496.0 42.3 %collective-permute-done.36 = bf16[1,128,2048]{2,1,0:T(8,128)(2,1)S(1)} collective-permute-done((bf16[1,128,2048]{2,1,0:T(8,128)(2,1)S(1)}, bf16[1,128,2048]{2,1,0:T(8,128)(2,1)S(1)}, u32[]{:S(2)}, u32[]{:S(2)}) %collective-permute-start.36) | collective-permute-done | bytes 524320 | tf_op jit(solution)/shard_map/ppermute | solution.py:71
  1538.4 45.8 %collective-permute-start.30 = (bf16[1,256,2048]{2,1,0:T(8,128)(2,1)S(1)}, bf16[1,256,2048]{2,1,0:T(8,128)(2,1)}, u32[]{:S(2)}, u32[]{:S(2)}) collective-permute-start(bf16[1,256,2048]{2,1,0:T(8,128)(2,1)S(1)} %get-tuple-element.117), channel_id=1, source_target_pairs={{0,6},{2,0},{4,2},{6,4},{1,7},{3,1},{5,3},{7,5},{8,14},{10,8},{12,... | collective-permute-start | bytes 3145736 | tf_op jit(solution)/shard_map/ppermute | solution.py:71
  1587.9 4.3 collective-permute-done.29
  1594.5 15.8 collective-permute-done.30
  1612.6 6.9 copy.279
  1619.5 8.2 copy.280
  1627.7 8.8 copy.285
  1636.5 14.2 fusion.32
  1650.8 47.8 %all-gather.1 = f32[32,1,4352]{2,1,0:T(1,128)} all-gather(f32[1,1,4352]{2,1,0:T(1,128)S(1)} %reshape.376), channel_id=2, replica_groups=mesh['y'=2,'c'=2,'a'=4,'b'=2] {'a','b','y','c'}, dimensions={0}, use_global_device_ids=true | all-gather | bytes 574464 | tf_op jit(solution)/shard_map/all_gather | solution.py:386
  1704.6 6.2 psum.7
  1714.4 5.3 convert_element_type.397
  (376 shorter events, 220.7 us)
Async XLA Ops:
  7.2 40.3 %copy-start.57 = (f32[2048]{0:T(1024)S(1)}, f32[2048]{0:T(1024)}, u32[]{:S(2)}) copy-start(f32[2048]{0:T(1024)} %param.15) | copy-start | bytes 24580
  7.2 162.0 %all-gather.9.cloned.1.call-start = ((), (), s32[]{:S(2)}) async-start(), calls=%async_computation.5 | async-start | bytes 25952256 | tf_op jit(solution)/shard_map/all_gather | solution.py:166
  10.0 238.1 %all-gather.11.cloned.1.call-start = ((), (), s32[]{:S(2)}) async-start(), calls=%async_computation.6 | async-start | bytes 8650752 | tf_op jit(solution)/shard_map/all_gather | solution.py:169
  11.8 612.3 %all-gather.13.cloned.1.call-start = ((), (), s32[]{:S(2)}) async-start(), calls=%async_computation.7 | async-start | bytes 10027008 | tf_op jit(solution)/shard_map/all_gather | solution.py:273
  11.9 249.4 %copy-start.55 = (bf16[2176]{0:T(1024)(128)(2,1)}, bf16[2176]{0:T(1024)(128)(2,1)S(1)}, u32[]{:S(2)}) copy-start(bf16[2176]{0:T(1024)(128)(2,1)S(1)} %pad.58.clone) | copy-start | bytes 13060
  44.7 211.8 %copy-start.40 = (bf16[2048,16]{0,1:T(8,128)(2,1)}, bf16[2048,16]{0,1:T(8,128)(2,1)S(1)}, u32[]{:S(2)}) copy-start(bf16[2048,16]{0,1:T(8,128)(2,1)S(1)} %all_gather.26) | copy-start | bytes 196612
  47.5 121.7 %copy-start.65 = (f32[256]{0:T(256)}, f32[256]{0:T(256)S(1)}, u32[]{:S(2)}) copy-start(f32[256]{0:T(256)S(1)} %add_rsqrt_fusion.3) | copy-start | bytes 3076
  49.1 120.2 %copy-start.30 = (bf16[256,2048]{1,0:T(8,128)(2,1)}, bf16[256,2048]{1,0:T(8,128)(2,1)S(1)}, u32[]{:S(2)}) copy-start(bf16[256,2048]{1,0:T(8,128)(2,1)S(1)} %fusion.27) | copy-start | bytes 3145732
  206.7 41.4 %copy-start.10 = (bf16[256,2048]{1,0:T(8,128)(2,1)S(1)}, bf16[256,2048]{1,0:T(8,128)(2,1)}, u32[]{:S(2)}) copy-start(bf16[256,2048]{1,0:T(8,128)(2,1)} %param.13) | copy-start | bytes 3145732
  263.9 408.9 %all-gather.15.cloned.1.call-start = ((), (), s32[]{:S(2)}) async-start(), calls=%async_computation.9 | async-start | bytes 9437184 | tf_op jit(solution)/shard_map/all_gather | solution.py:217
  281.4 50.6 %collective-permute-start = (bf16[1,256,2048]{2,1,0:T(8,128)(2,1)}, bf16[1,256,2048]{2,1,0:T(8,128)(2,1)}, u32[]{:S(2)}, u32[]{:S(2)}) collective-permute-start(bf16[1,256,2048]{2,1,0:T(8,128)(2,1)} %bitcast.346), channel_id=1, source_target_pairs={{0,2},{2,4},{4,6},{6,0},{1,3},{3,5},{5,7},{7,1},{8,10},{10,12},{12... | collective-permute-start | bytes 3145736 | tf_op jit(solution)/shard_map/ppermute | solution.py:71
  284.2 117.3 %collective-permute-start.1 = (bf16[1,256,2048]{2,1,0:T(8,128)(2,1)}, bf16[1,256,2048]{2,1,0:T(8,128)(2,1)}, u32[]{:S(2)}, u32[]{:S(2)}) collective-permute-start(bf16[1,256,2048]{2,1,0:T(8,128)(2,1)} %bitcast.345), channel_id=1, source_target_pairs={{0,4},{2,6},{4,0},{6,2},{1,5},{3,7},{5,1},{7,3},{8,12},{10,14},{12... | collective-permute-start | bytes 3145736 | tf_op jit(solution)/shard_map/ppermute | solution.py:71
  286.5 117.3 %collective-permute-start.2 = (bf16[1,256,2048]{2,1,0:T(8,128)(2,1)}, bf16[1,256,2048]{2,1,0:T(8,128)(2,1)S(1)}, u32[]{:S(2)}, u32[]{:S(2)}) collective-permute-start(bf16[1,256,2048]{2,1,0:T(8,128)(2,1)} %bitcast.344), channel_id=1, source_target_pairs={{0,6},{2,0},{4,2},{6,4},{1,7},{3,1},{5,3},{7,5},{8,14},{10,8},{12,... | collective-permute-start | bytes 3145736 | tf_op jit(solution)/shard_map/ppermute | solution.py:71
  291.5 134.8 %collective-permute-start.4 = (bf16[1,128,2048]{2,1,0:T(8,128)(2,1)}, bf16[1,128,2048]{2,1,0:T(8,128)(2,1)}, u32[]{:S(2)}, u32[]{:S(2)}) collective-permute-start(bf16[1,128,2048]{2,1,0:T(8,128)(2,1)} %get-tuple-element.141), channel_id=1, source_target_pairs={{0,2},{2,4},{4,6},{6,0},{1,3},{3,5},{5,7},{7,1},{8,10},{10,12},{12... | collective-permute-start | bytes 1572872 | tf_op jit(solution)/shard_map/ppermute | solution.py:71
  291.5 191.2 %collective-permute-start.5 = (bf16[1,128,2048]{2,1,0:T(8,128)(2,1)}, bf16[1,128,2048]{2,1,0:T(8,128)(2,1)}, u32[]{:S(2)}, u32[]{:S(2)}) collective-permute-start(bf16[1,128,2048]{2,1,0:T(8,128)(2,1)} %get-tuple-element.142), channel_id=1, source_target_pairs={{0,4},{2,6},{4,0},{6,2},{1,5},{3,7},{5,1},{7,3},{8,12},{10,14},{12... | collective-permute-start | bytes 1572872 | tf_op jit(solution)/shard_map/ppermute | solution.py:71
  293.2 640.2 %reduce-scatter.8.cloned.1.call-start = ((), (), s32[]{:S(2)}) async-start(), calls=%async_computation.10 | async-start | bytes 10027008 | tf_op jit(solution)/shard_map/reduce_scatter | solution.py:304
  331.9 151.8 %collective-permute-start.6 = (bf16[1,128,2048]{2,1,0:T(8,128)(2,1)}, bf16[1,128,2048]{2,1,0:T(8,128)(2,1)S(1)}, u32[]{:S(2)}, u32[]{:S(2)}) collective-permute-start(bf16[1,128,2048]{2,1,0:T(8,128)(2,1)} %get-tuple-element.140), channel_id=1, source_target_pairs={{0,6},{2,0},{4,2},{6,4},{1,7},{3,1},{5,3},{7,5},{8,14},{10,8},{12,... | collective-permute-start | bytes 1572872 | tf_op jit(solution)/shard_map/ppermute | solution.py:71
  404.9 143.0 %collective-permute-start.3 = (bf16[1024,2048]{1,0:T(8,128)(2,1)}, bf16[1024,2048]{1,0:T(8,128)(2,1)}, u32[]{:S(2)}, u32[]{:S(2)}) collective-permute-start(bf16[1024,2048]{1,0:T(8,128)(2,1)} %bitcast.17), channel_id=1, source_target_pairs={{0,1},{1,0},{2,3},{3,2},{4,5},{5,4},{6,7},{7,6},{8,9},{9,8},{10,11... | collective-permute-start | bytes 12582920 | tf_op jit(solution)/shard_map/ppermute | solution.py:71
  406.2 144.2 %collective-permute-start.8 = (bf16[1024,2048]{1,0:T(8,128)(2,1)}, bf16[1024,2048]{1,0:T(8,128)(2,1)}, u32[]{:S(2)}, u32[]{:S(2)}) collective-permute-start(bf16[1024,2048]{1,0:T(8,128)(2,1)} %bitcast.17), channel_id=1, source_target_pairs={{0,16},{16,0},{1,17},{17,1},{2,18},{18,2},{3,19},{19,3},{4,20},{20... | collective-permute-start | bytes 12582920 | tf_op jit(solution)/shard_map/ppermute | solution.py:71
  483.8 58.6 %collective-permute-start.7 = (bf16[512,2048]{1,0:T(8,128)(2,1)S(1)}, bf16[512,2048]{1,0:T(8,128)(2,1)S(1)}, u32[]{:S(2)}, u32[]{:S(2)}) collective-permute-start(bf16[512,2048]{1,0:T(8,128)(2,1)S(1)} %bitcast.311), channel_id=1, source_target_pairs={{0,1},{1,0},{2,3},{3,2},{4,5},{5,4},{6,7},{7,6},{8,9},{9,8},{10,11... | collective-permute-start | bytes 6291464 | tf_op jit(solution)/shard_map/ppermute | solution.py:71
  485.3 58.7 %collective-permute-start.11 = (bf16[512,2048]{1,0:T(8,128)(2,1)S(1)}, bf16[512,2048]{1,0:T(8,128)(2,1)S(1)}, u32[]{:S(2)}, u32[]{:S(2)}) collective-permute-start(bf16[512,2048]{1,0:T(8,128)(2,1)S(1)} %bitcast.312), channel_id=1, source_target_pairs={{0,16},{16,0},{1,17},{17,1},{2,18},{18,2},{3,19},{19,3},{4,20},{20... | collective-permute-start | bytes 6291464 | tf_op jit(solution)/shard_map/ppermute | solution.py:71
  542.5 26.3 %collective-permute-start.13 = (bf16[256,2048]{1,0:T(8,128)(2,1)S(1)}, bf16[256,2048]{1,0:T(8,128)(2,1)}, u32[]{:S(2)}, u32[]{:S(2)}) collective-permute-start(bf16[256,2048]{1,0:T(8,128)(2,1)S(1)} %slice.308), channel_id=1, source_target_pairs={{0,16},{16,0},{1,17},{17,1},{2,18},{18,2},{3,19},{19,3},{4,20},{20... | collective-permute-start | bytes 3145736 | tf_op jit(solution)/shard_map/ppermute | solution.py:71
  546.4 26.4 %collective-permute-start.12 = (bf16[256,2048]{1,0:T(8,128)(2,1)}, bf16[256,2048]{1,0:T(8,128)(2,1)}, u32[]{:S(2)}, u32[]{:S(2)}) collective-permute-start(bf16[256,2048]{1,0:T(8,128)(2,1)} %slice.307), channel_id=1, source_target_pairs={{0,1},{1,0},{2,3},{3,2},{4,5},{5,4},{6,7},{7,6},{8,9},{9,8},{10,11... | collective-permute-start | bytes 3145736 | tf_op jit(solution)/shard_map/ppermute | solution.py:71
  549.7 62.0 %collective-permute-start.10 = (bf16[512,2048]{1,0:T(8,128)(2,1)S(1)}, bf16[512,2048]{1,0:T(8,128)(2,1)S(1)}, u32[]{:S(2)}, u32[]{:S(2)}) collective-permute-start(bf16[512,2048]{1,0:T(8,128)(2,1)S(1)} %slice.304), channel_id=1, source_target_pairs={{0,16},{16,0},{1,17},{17,1},{2,18},{18,2},{3,19},{19,3},{4,20},{20... | collective-permute-start | bytes 6291464 | tf_op jit(solution)/shard_map/ppermute | solution.py:71
  552.1 63.4 %collective-permute-start.9 = (bf16[512,2048]{1,0:T(8,128)(2,1)S(1)}, bf16[512,2048]{1,0:T(8,128)(2,1)S(1)}, u32[]{:S(2)}, u32[]{:S(2)}) collective-permute-start(bf16[512,2048]{1,0:T(8,128)(2,1)S(1)} %slice.303), channel_id=1, source_target_pairs={{0,1},{1,0},{2,3},{3,2},{4,5},{5,4},{6,7},{7,6},{8,9},{9,8},{10,11... | collective-permute-start | bytes 6291464 | tf_op jit(solution)/shard_map/ppermute | solution.py:71
  553.3 70.8 %copy-start.71 = (f32[16]{0:T(128)}, f32[16]{0:T(128)S(1)}, u32[]{:S(2)}) copy-start(f32[16]{0:T(128)S(1)} %get-tuple-element.175) | copy-start | bytes 196
  553.3 70.8 %copy-start.73 = (f32[16]{0:T(128)}, f32[16]{0:T(128)S(1)}, u32[]{:S(2)}) copy-start(f32[16]{0:T(128)S(1)} %get-tuple-element.176) | copy-start | bytes 196
  625.1 157.8 %copy-start.69 = (f32[2048]{0:T(1024)}, f32[2048]{0:T(1024)S(1)}, u32[]{:S(2)}) copy-start(f32[2048]{0:T(1024)S(1)} %get-tuple-element.78) | copy-start | bytes 24580
  782.8 241.3 %reduce-scatter.6.cloned.1.call-start = ((), (), s32[]{:S(2)}) async-start(), calls=%async_computation.8 | async-start | bytes 9437184 | tf_op jit(solution)/shard_map/reduce_scatter | solution.py:305
  816.4 665.6 %reduce-scatter.12.cloned.1.call-start = ((), (), s32[]{:S(2)}) async-start(), calls=%async_computation.13 | async-start | bytes 1310720 | tf_op jit(solution)/shard_map/reduce_scatter | solution.py:134
  941.0 83.1 %copy-start.24 = (bf16[256,2048]{1,0:T(8,128)(2,1)S(1)}, bf16[256,2048]{1,0:T(8,128)(2,1)}, u32[]{:S(2)}) copy-start(bf16[256,2048]{1,0:T(8,128)(2,1)} %param.24) | copy-start | bytes 3145732
  1062.1 63.3 %collective-permute-start.14 = (bf16[1024,6144]{1,0:T(8,128)(2,1)}, bf16[1024,6144]{1,0:T(8,128)(2,1)}, u32[]{:S(2)}, u32[]{:S(2)}) collective-permute-start(bf16[1024,6144]{1,0:T(8,128)(2,1)} %convolution_convert_fusion), channel_id=1, source_target_pairs={{0,8},{8,0},{1,9},{9,1},{2,10},{10,2},{3,11},{11,3},{4,12},{12,4},... | collective-permute-start | bytes 37748744 | tf_op jit(solution)/shard_map/ppermute | solution.py:71
  1063.5 55.3 %collective-permute-start.19 = (bf16[1024,2048]{1,0:T(8,128)(2,1)S(1)}, bf16[1024,2048]{1,0:T(8,128)(2,1)S(1)}, u32[]{:S(2)}, u32[]{:S(2)}) collective-permute-start(bf16[1024,2048]{1,0:T(8,128)(2,1)S(1)} %convolution_convert_fusion.5), channel_id=1, source_target_pairs={{0,8},{8,0},{1,9},{9,1},{2,10},{10,2},{3,11},{11,3},{4,12},{12,4},... | collective-permute-start | bytes 12582920 | tf_op jit(solution)/shard_map/ppermute | solution.py:71
  1093.4 207.1 %collective-permute-start.26 = (bf16[512,2048]{1,0:T(8,128)(2,1)}, bf16[512,2048]{1,0:T(8,128)(2,1)}, u32[]{:S(2)}, u32[]{:S(2)}) collective-permute-start(bf16[512,2048]{1,0:T(8,128)(2,1)} %get-tuple-element.110), channel_id=1, source_target_pairs={{0,16},{16,0},{1,17},{17,1},{2,18},{18,2},{3,19},{19,3},{4,20},{20... | collective-permute-start | bytes 6291464 | tf_op jit(solution)/shard_map/ppermute | solution.py:71
  1123.4 31.1 %collective-permute-start.20 = (bf16[128,2048]{1,0:T(8,128)(2,1)}, bf16[128,2048]{1,0:T(8,128)(2,1)}, u32[]{:S(2)}, u32[]{:S(2)}) collective-permute-start(bf16[128,2048]{1,0:T(8,128)(2,1)} %get-tuple-element.123), channel_id=1, source_target_pairs={{0,1},{1,0},{2,3},{3,2},{4,5},{5,4},{6,7},{7,6},{8,9},{9,8},{10,11... | collective-permute-start | bytes 1572872 | tf_op jit(solution)/shard_map/ppermute | solution.py:71
  1124.9 29.6 %collective-permute-start.22 = (bf16[128,2048]{1,0:T(8,128)(2,1)}, bf16[128,2048]{1,0:T(8,128)(2,1)}, u32[]{:S(2)}, u32[]{:S(2)}) collective-permute-start(bf16[128,2048]{1,0:T(8,128)(2,1)} %get-tuple-element.125), channel_id=1, source_target_pairs={{0,16},{16,0},{1,17},{17,1},{2,18},{18,2},{3,19},{19,3},{4,20},{20... | collective-permute-start | bytes 1572872 | tf_op jit(solution)/shard_map/ppermute | solution.py:71
  1138.6 37.4 %collective-permute-start.15 = (bf16[128,6144]{1,0:T(8,128)(2,1)S(1)}, bf16[128,6144]{1,0:T(8,128)(2,1)S(1)}, u32[]{:S(2)}, u32[]{:S(2)}) collective-permute-start(bf16[128,6144]{1,0:T(8,128)(2,1)S(1)} %get-tuple-element.105), channel_id=1, source_target_pairs={{0,1},{1,0},{2,3},{3,2},{4,5},{5,4},{6,7},{7,6},{8,9},{9,8},{10,11... | collective-permute-start | bytes 4718600 | tf_op jit(solution)/shard_map/ppermute | solution.py:71
  1139.2 47.9 %collective-permute-start.17 = (bf16[128,6144]{1,0:T(8,128)(2,1)S(1)}, bf16[128,6144]{1,0:T(8,128)(2,1)S(1)}, u32[]{:S(2)}, u32[]{:S(2)}) collective-permute-start(bf16[128,6144]{1,0:T(8,128)(2,1)S(1)} %get-tuple-element.107), channel_id=1, source_target_pairs={{0,16},{16,0},{1,17},{17,1},{2,18},{18,2},{3,19},{19,3},{4,20},{20... | collective-permute-start | bytes 4718600 | tf_op jit(solution)/shard_map/ppermute | solution.py:71
  1154.5 57.6 %copy-start.29 = (bf16[1024,2048]{1,0:T(8,128)(2,1)}, bf16[1024,2048]{1,0:T(8,128)(2,1)S(1)}, u32[]{:S(2)}) copy-start(bf16[1024,2048]{1,0:T(8,128)(2,1)S(1)} %convolution_convert_fusion.3) | copy-start | bytes 12582916
  1157.1 56.9 %collective-permute-start.23 = (bf16[256,2048]{1,0:T(8,128)(2,1)S(1)}, bf16[256,2048]{1,0:T(8,128)(2,1)S(1)}, u32[]{:S(2)}, u32[]{:S(2)}) collective-permute-start(bf16[256,2048]{1,0:T(8,128)(2,1)S(1)} %pad_maximum_fusion.14), channel_id=1, source_target_pairs={{0,1},{1,0},{2,3},{3,2},{4,5},{5,4},{6,7},{7,6},{8,9},{9,8},{10,11... | collective-permute-start | bytes 3145736 | tf_op jit(solution)/shard_map/ppermute | solution.py:71
  1158.7 55.8 %collective-permute-start.21 = (bf16[256,2048]{1,0:T(8,128)(2,1)S(1)}, bf16[256,2048]{1,0:T(8,128)(2,1)S(1)}, u32[]{:S(2)}, u32[]{:S(2)}) collective-permute-start(bf16[256,2048]{1,0:T(8,128)(2,1)S(1)} %pad_maximum_fusion.13), channel_id=1, source_target_pairs={{0,16},{16,0},{1,17},{17,1},{2,18},{18,2},{3,19},{19,3},{4,20},{20... | collective-permute-start | bytes 3145736 | tf_op jit(solution)/shard_map/ppermute | solution.py:71
  1192.1 73.8 %collective-permute-start.18 = (bf16[256,6144]{1,0:T(8,128)(2,1)}, bf16[256,6144]{1,0:T(8,128)(2,1)}, u32[]{:S(2)}, u32[]{:S(2)}) collective-permute-start(bf16[256,6144]{1,0:T(8,128)(2,1)} %pad_maximum_fusion.10), channel_id=1, source_target_pairs={{0,1},{1,0},{2,3},{3,2},{4,5},{5,4},{6,7},{7,6},{8,9},{9,8},{10,11... | collective-permute-start | bytes 9437192 | tf_op jit(solution)/shard_map/ppermute | solution.py:71
  1195.6 81.5 %collective-permute-start.16 = (bf16[256,6144]{1,0:T(8,128)(2,1)}, bf16[256,6144]{1,0:T(8,128)(2,1)}, u32[]{:S(2)}, u32[]{:S(2)}) collective-permute-start(bf16[256,6144]{1,0:T(8,128)(2,1)} %pad_maximum_fusion.9), channel_id=1, source_target_pairs={{0,16},{16,0},{1,17},{17,1},{2,18},{18,2},{3,19},{19,3},{4,20},{20... | collective-permute-start | bytes 9437192 | tf_op jit(solution)/shard_map/ppermute | solution.py:71
  1214.0 96.9 %collective-permute-start.24 = (bf16[512,2048]{1,0:T(8,128)(2,1)}, bf16[512,2048]{1,0:T(8,128)(2,1)}, u32[]{:S(2)}, u32[]{:S(2)}) collective-permute-start(bf16[512,2048]{1,0:T(8,128)(2,1)} %get-tuple-element.109), channel_id=1, source_target_pairs={{0,1},{1,0},{2,3},{3,2},{4,5},{5,4},{6,7},{7,6},{8,9},{9,8},{10,11... | collective-permute-start | bytes 6291464 | tf_op jit(solution)/shard_map/ppermute | solution.py:71
  1214.5 84.1 %collective-permute-start.33 = (bf16[256,2048]{1,0:T(8,128)(2,1)}, bf16[256,2048]{1,0:T(8,128)(2,1)}, u32[]{:S(2)}, u32[]{:S(2)}) collective-permute-start(bf16[256,2048]{1,0:T(8,128)(2,1)} %get-tuple-element.115), channel_id=1, source_target_pairs={{0,16},{16,0},{1,17},{17,1},{2,18},{18,2},{3,19},{19,3},{4,20},{20... | collective-permute-start | bytes 3145736 | tf_op jit(solution)/shard_map/ppermute | solution.py:71
  1216.7 371.2 %reduce-scatter.10.cloned.1.call-start = ((), (), s32[]{:S(2)}) async-start(), calls=%async_computation.11 | async-start | bytes 3932160 | tf_op jit(solution)/shard_map/reduce_scatter | solution.py:134
  1266.0 67.4 %collective-permute-start.31 = (bf16[256,2048]{1,0:T(8,128)(2,1)}, bf16[256,2048]{1,0:T(8,128)(2,1)}, u32[]{:S(2)}, u32[]{:S(2)}) collective-permute-start(bf16[256,2048]{1,0:T(8,128)(2,1)} %get-tuple-element.114), channel_id=1, source_target_pairs={{0,1},{1,0},{2,3},{3,2},{4,5},{5,4},{6,7},{7,6},{8,9},{9,8},{10,11... | collective-permute-start | bytes 3145736 | tf_op jit(solution)/shard_map/ppermute | solution.py:71
  1284.2 420.4 %reduce-scatter.14.cloned.1.call-start = ((), (), s32[]{:S(2)}) async-start(), calls=%async_computation.15 | async-start | bytes 73728 | tf_op jit(solution)/shard_map/reduce_scatter | solution.py:347
  1306.3 165.6 %collective-permute-start.27 = (bf16[1024,2048]{1,0:T(8,128)(2,1)}, bf16[1024,2048]{1,0:T(8,128)(2,1)}, u32[]{:S(2)}, u32[]{:S(2)}) collective-permute-start(bf16[1024,2048]{1,0:T(8,128)(2,1)} %pad_maximum_fusion.7), channel_id=1, source_target_pairs={{0,1},{1,0},{2,3},{3,2},{4,5},{5,4},{6,7},{7,6},{8,9},{9,8},{10,11... | collective-permute-start | bytes 12582920 | tf_op jit(solution)/shard_map/ppermute | solution.py:71
  1316.6 155.3 %collective-permute-start.25 = (bf16[1024,2048]{1,0:T(8,128)(2,1)}, bf16[1024,2048]{1,0:T(8,128)(2,1)}, u32[]{:S(2)}, u32[]{:S(2)}) collective-permute-start(bf16[1024,2048]{1,0:T(8,128)(2,1)} %pad_maximum_fusion.6), channel_id=1, source_target_pairs={{0,16},{16,0},{1,17},{17,1},{2,18},{18,2},{3,19},{19,3},{4,20},{20... | collective-permute-start | bytes 12582920 | tf_op jit(solution)/shard_map/ppermute | solution.py:71
  1318.4 147.8 %copy-start.32 = (bf16[1024,2048]{1,0:T(8,128)(2,1)S(1)}, bf16[1024,2048]{1,0:T(8,128)(2,1)}, u32[]{:S(2)}) copy-start(bf16[1024,2048]{1,0:T(8,128)(2,1)} %convolution_convert_fusion.4) | copy-start | bytes 12582916
  1318.4 147.8 %collective-permute-start.34 = (bf16[512,2048]{1,0:T(8,128)(2,1)S(1)}, bf16[512,2048]{1,0:T(8,128)(2,1)S(1)}, u32[]{:S(2)}, u32[]{:S(2)}) collective-permute-start(bf16[512,2048]{1,0:T(8,128)(2,1)S(1)} %pad_maximum_fusion.12), channel_id=1, source_target_pairs={{0,1},{1,0},{2,3},{3,2},{4,5},{5,4},{6,7},{7,6},{8,9},{9,8},{10,11... | collective-permute-start | bytes 6291464 | tf_op jit(solution)/shard_map/ppermute | solution.py:71
  1335.6 134.7 %copy-start.15 = (bf16[256,2048]{1,0:T(8,128)(2,1)S(1)}, bf16[256,2048]{1,0:T(8,128)(2,1)}, u32[]{:S(2)}) copy-start(bf16[256,2048]{1,0:T(8,128)(2,1)} %copy-done.14) | copy-start | bytes 3145732
  1335.6 134.7 %copy-start.48 = (f32[256,16]{0,1:T(8,128)S(1)}, f32[256,16]{0,1:T(8,128)}, u32[]{:S(2)}) copy-start(f32[256,16]{0,1:T(8,128)} %copy-done.46) | copy-start | bytes 49156
  1335.6 134.7 %copy-start.68 = (f32[256]{0:T(256)S(1)}, f32[256]{0:T(256)}, u32[]{:S(2)}) copy-start(f32[256]{0:T(256)} %copy-done.67) | copy-start | bytes 3076
  1335.6 130.7 %collective-permute-start.32 = (bf16[512,2048]{1,0:T(8,128)(2,1)S(1)}, bf16[512,2048]{1,0:T(8,128)(2,1)S(1)}, u32[]{:S(2)}, u32[]{:S(2)}) collective-permute-start(bf16[512,2048]{1,0:T(8,128)(2,1)S(1)} %pad_maximum_fusion.11), channel_id=1, source_target_pairs={{0,16},{16,0},{1,17},{17,1},{2,18},{18,2},{3,19},{19,3},{4,20},{20... | collective-permute-start | bytes 6291464 | tf_op jit(solution)/shard_map/ppermute | solution.py:71
  1470.2 24.7 %collective-permute-start.35 = (bf16[1,128,2048]{2,1,0:T(8,128)(2,1)}, bf16[1,128,2048]{2,1,0:T(8,128)(2,1)}, u32[]{:S(2)}, u32[]{:S(2)}) collective-permute-start(bf16[1,128,2048]{2,1,0:T(8,128)(2,1)} %get-tuple-element.133), channel_id=1, source_target_pairs={{0,2},{2,4},{4,6},{6,0},{1,3},{3,5},{5,7},{7,1},{8,10},{10,12},{12... | collective-permute-start | bytes 1572872 | tf_op jit(solution)/shard_map/ppermute | solution.py:71
  1471.9 239.6 %all-gather.19.cloned.1.call-start = ((), (), s32[]{:S(2)}) async-start(), calls=%async_computation.14 | async-start | bytes 1310720 | tf_op jit(solution)/shard_map/all_gather | solution.py:135
  1482.0 232.4 %all-gather.17.cloned.1.call-start = ((), (), s32[]{:S(2)}) async-start(), calls=%async_computation.12 | async-start | bytes 3932160 | tf_op jit(solution)/shard_map/all_gather | solution.py:135
  1487.7 99.1 %collective-permute-start.28 = (bf16[1,256,2048]{2,1,0:T(8,128)(2,1)S(1)}, bf16[1,256,2048]{2,1,0:T(8,128)(2,1)S(1)}, u32[]{:S(2)}, u32[]{:S(2)}) collective-permute-start(bf16[1,256,2048]{2,1,0:T(8,128)(2,1)S(1)} %get-tuple-element.119), channel_id=1, source_target_pairs={{0,2},{2,4},{4,6},{6,0},{1,3},{3,5},{5,7},{7,1},{8,10},{10,12},{12... | collective-permute-start | bytes 3145736 | tf_op jit(solution)/shard_map/ppermute | solution.py:71
  1488.8 49.5 %collective-permute-start.36 = (bf16[1,128,2048]{2,1,0:T(8,128)(2,1)S(1)}, bf16[1,128,2048]{2,1,0:T(8,128)(2,1)S(1)}, u32[]{:S(2)}, u32[]{:S(2)}) collective-permute-start(bf16[1,128,2048]{2,1,0:T(8,128)(2,1)S(1)} %copy-done.45), channel_id=1, source_target_pairs={{0,4},{2,6},{4,0},{6,2},{1,5},{3,7},{5,1},{7,3},{8,12},{10,14},{12... | collective-permute-start | bytes 1572872 | tf_op jit(solution)/shard_map/ppermute | solution.py:71
  1492.1 92.1 %collective-permute-start.37 = (bf16[1,128,2048]{2,1,0:T(8,128)(2,1)S(1)}, bf16[1,128,2048]{2,1,0:T(8,128)(2,1)S(1)}, u32[]{:S(2)}, u32[]{:S(2)}) collective-permute-start(bf16[1,128,2048]{2,1,0:T(8,128)(2,1)S(1)} %copy-done.44), channel_id=1, source_target_pairs={{0,6},{2,0},{4,2},{6,4},{1,7},{3,1},{5,3},{7,5},{8,14},{10,8},{12,... | collective-permute-start | bytes 1572872 | tf_op jit(solution)/shard_map/ppermute | solution.py:71
  1493.4 98.8 %collective-permute-start.29 = (bf16[1,256,2048]{2,1,0:T(8,128)(2,1)}, bf16[1,256,2048]{2,1,0:T(8,128)(2,1)}, u32[]{:S(2)}, u32[]{:S(2)}) collective-permute-start(bf16[1,256,2048]{2,1,0:T(8,128)(2,1)} %get-tuple-element.118), channel_id=1, source_target_pairs={{0,4},{2,6},{4,0},{6,2},{1,5},{3,7},{5,1},{7,3},{8,12},{10,14},{12... | collective-permute-start | bytes 3145736 | tf_op jit(solution)/shard_map/ppermute | solution.py:71
  1538.4 71.9 %collective-permute-start.30 = (bf16[1,256,2048]{2,1,0:T(8,128)(2,1)S(1)}, bf16[1,256,2048]{2,1,0:T(8,128)(2,1)}, u32[]{:S(2)}, u32[]{:S(2)}) collective-permute-start(bf16[1,256,2048]{2,1,0:T(8,128)(2,1)S(1)} %get-tuple-element.117), channel_id=1, source_target_pairs={{0,6},{2,0},{4,2},{6,4},{1,7},{3,1},{5,3},{7,5},{8,14},{10,8},{12,... | collective-permute-start | bytes 3145736 | tf_op jit(solution)/shard_map/ppermute | solution.py:71
  (67 other events, 489.2 us)
Sparse Core Ops, SparseCore 0:
  11.5 157.6 all-gather.8
  172.7 75.3 all-gather.10
  264.1 188.2 all-gather.12
  453.8 97.0 all-gather.14
  782.9 150.4 reduce-scatter.7
  936.1 87.9 reduce-scatter.5
  1216.8 25.4 reduce-scatter.11
  1284.4 58.6 reduce-scatter.9
  1472.0 127.5 reduce-scatter.13
  1601.1 16.2 all-gather.18
  1619.0 28.5 all-gather.16
